TPU v7x, 512 devices: a whole 4x4x16 slice. The times are simulated.
512 devices in a mesh: row: 32 (over y_lo, z), col: 16 (over y_hi, x, core).
Axes of the slice: x: 4, y: 4 (y_hi: 2, y_lo: 2; y = y_hi * 2 + y_lo), z: 16, core: 2. Of those that a mesh axis runs over, the one named last changes fastest.
Arguments:
- image: bfloat16 [32, 2048, 2048], P(None, 'row', 'col'), may hold values from -6 to 6
- weight: bfloat16 [3, 3, 32, 32], replicated, may hold values from -0.375 to 0.375
- bias: float32 [32], replicated, may hold values from -3 to 3
- cotangent: bfloat16 [32, 2048, 2048], P(None, 'row', 'col'), may hold values from -60 to 60
Outputs:
- activation: bfloat16 [32, 2048, 2048], P(None, 'row', 'col')
- grad_image: bfloat16 [32, 2048, 2048], P(None, 'row', 'col')
- grad_weight: float32 [3, 3, 32, 32], replicated
- grad_bias: float32 [32], replicated
All inputs are finite; a program needn't handle non-finite values.
Results may differ from a plain program's by a relative error of at most 0.0065.
Values may be sent and summed in bfloat16 or wider, within the bound.
A program may use at most 64 MiB of HBM per device.

v0:
```python
import math

import jax
import jax.numpy as jnp
from jax import lax
from jax.sharding import PartitionSpec as P

DILATION_PIXELS = 16


def from_behind(value, axis, steps):
    count = lax.axis_size(axis)
    initial, last = (max(0, -steps), min(count, count - steps))
    return lax.ppermute(value, axis, [(source, source + steps) for source in range(initial, last)])


def gelu_pair(preact):
    coef = 0.7978845608
    cube = preact * preact * preact
    tval = jnp.tanh(coef * (preact + 0.044715 * cube))
    value = 0.5 * preact * (1.0 + tval)
    slope_val = 0.5 * (1.0 + tval) + 0.5 * preact * (1.0 - tval * tval) * coef * (
        1.0 + 3.0 * 0.044715 * preact * preact
    )
    return (value, slope_val)


def extended(local_block):
    row_count = local_block.shape[1]
    column_count = local_block.shape[2]
    upper_neighbour = from_behind(local_block[:, row_count - DILATION_PIXELS :, :], "row", 1)
    lower_neighbour = from_behind(local_block[:, :DILATION_PIXELS, :], "row", -1)
    tall_block = jnp.concatenate([upper_neighbour, local_block, lower_neighbour], axis=1)
    left_margin = from_behind(tall_block[:, :, column_count - DILATION_PIXELS :], "col", 1)
    right_margin = from_behind(tall_block[:, :, :DILATION_PIXELS], "col", -1)
    return jnp.concatenate([left_margin, tall_block, right_margin], axis=2)


def tap_view(ext, row_offset, column_offset, row_count, column_count):
    start_row = DILATION_PIXELS + row_offset * DILATION_PIXELS
    start_column = DILATION_PIXELS + column_offset * DILATION_PIXELS
    return ext[:, start_row : start_row + row_count, start_column : start_column + column_count]


def row_stack(ext, row_offset, sign_flip, row_count, column_count):
    return jnp.concatenate(
        [
            tap_view(
                ext, sign_flip * row_offset, sign_flip * column_offset, row_count, column_count
            )
            for column_offset in (-1, 0, 1)
        ],
        axis=0,
    )


def shards(image, weight, bias, cotangent):
    row_count = image.shape[1]
    column_count = image.shape[2]
    channels = image.shape[0]
    height_all = row_count * lax.axis_size("row")
    width_all = column_count * lax.axis_size("col")
    scale = 1.0 / math.sqrt(height_all * width_all)
    image_ext = extended(image)
    preact = jnp.zeros(image.shape, jnp.float32) + bias[:, None, None]
    for row_offset in (-1, 0, 1):
        weight_row = jnp.transpose(weight[row_offset + 1], (1, 0, 2)).reshape(
            channels, 3 * channels
        )
        stacked = row_stack(image_ext, row_offset, 1, row_count, column_count)
        preact = preact + jnp.einsum(
            "ok,krq->orq", weight_row, stacked, preferred_element_type=jnp.float32
        )
    value, slope_val = gelu_pair(preact)
    activation = value.astype(jnp.bfloat16)
    preact_gradient = (cotangent.astype(jnp.float32) * slope_val).astype(jnp.bfloat16)
    taps = []
    for row_offset in (-1, 0, 1):
        stacked = row_stack(image_ext, row_offset, 1, row_count, column_count)
        joined = (
            jnp.einsum("orq,krq->ok", preact_gradient, stacked, preferred_element_type=jnp.float32)
            * scale
        )
        taps.append(jnp.transpose(joined.reshape(channels, 3, channels), (1, 0, 2)))
    local_weight = jnp.stack(taps)
    local_bias = jnp.sum(preact_gradient.astype(jnp.float32), axis=(1, 2)) * scale
    grad_weight, grad_bias = lax.psum((local_weight, local_bias), ("row", "col"))
    grad_ext = extended(preact_gradient)
    total = jnp.zeros(image.shape, jnp.float32)
    for row_offset in (-1, 0, 1):
        weight_row = weight[row_offset + 1].reshape(3 * channels, channels)
        stacked = row_stack(grad_ext, row_offset, -1, row_count, column_count)
        total = total + jnp.einsum(
            "kc,krq->crq", weight_row, stacked, preferred_element_type=jnp.float32
        )
    grad_image = total.astype(jnp.bfloat16)
    return (activation, grad_image, grad_weight, grad_bias)


def solution(mesh):
    return jax.shard_map(
        shards,
        mesh=mesh,
        in_specs=(P(None, "row", "col"), P(), P(), P(None, "row", "col")),
        out_specs=(P(None, "row", "col"), P(None, "row", "col"), P(), P()),
        check_vma=False,
    )
```

profile of v0, /device:TPU:1, one launch (start us, length us, event | category | flops | bytes accessed | tf_op | source)
XLA Modules:
  0.0 181.4 jit_solution(1297893469584585609)
XLA Ops:
  0.6 1.4 copy.42
  2.1 4.4 %collective-permute-start = (bf16[32,16,128]{2,0,1:T(8,128)(2,1)S(1)}, bf16[32,16,128]{2,0,1:T(8,128)(2,1)S(1)}, u32[]{:S(2)}, u32[]{:S(2)}) collective-permute-start(bf16[32,16,128]{2,0,1:T(8,128)(2,1)S(1)} %get-tuple-element.42), channel_id=1, source_target_pairs={{0,16},{16,32},{32,48},{48,64},{64,80},{80,96},{96,112},{112,128},... | collective-permute-start | bytes 393224 | tf_op jit(solution)/shard_map/ppermute | solution.py:14
  6.5 1.3 collective-permute-start.1
  7.8 0.6 collective-permute-done
  8.4 0.4 constant_dynamic-update-slice_fusion.1
  8.8 3.6 %collective-permute-done.1 = bf16[32,16,128]{2,0,1:T(8,128)(2,1)S(1)} collective-permute-done((bf16[32,16,128]{2,0,1:T(8,128)(2,1)S(1)}, bf16[32,16,128]{2,0,1:T(8,128)(2,1)S(1)}, u32[]{:S(2)}, u32[]{:S(2)}) %collective-permute-start.1) | collective-permute-done | bytes 131104 | tf_op jit(solution)/shard_map/ppermute | solution.py:14
  12.4 0.3 fusion.68
  12.7 0.8 copy.45
  13.5 0.8 copy.48
  14.4 6.6 %collective-permute-start.3 = (bf16[32,96,16]{1,2,0:T(8,128)(2,1)S(1)}, bf16[32,96,16]{1,2,0:T(8,128)(2,1)S(1)}, u32[]{:S(2)}, u32[]{:S(2)}) collective-permute-start(bf16[32,96,16]{1,2,0:T(8,128)(2,1)S(1)} %copy.48), channel_id=1, source_target_pairs={{1,0},{2,1},{3,2},{4,3},{5,4},{6,5},{7,6},{8,7},{9,8},{10,9},{11,1... | collective-permute-start | bytes 294920 | tf_op jit(solution)/shard_map/ppermute | solution.py:14
  21.0 1.9 %collective-permute-start.2 = (bf16[32,96,16]{1,2,0:T(8,128)(2,1)S(1)}, bf16[32,96,16]{1,2,0:T(8,128)(2,1)S(1)}, u32[]{:S(2)}, u32[]{:S(2)}) collective-permute-start(bf16[32,96,16]{1,2,0:T(8,128)(2,1)S(1)} %copy.45), channel_id=1, source_target_pairs={{0,1},{1,2},{2,3},{3,4},{4,5},{5,6},{6,7},{7,8},{8,9},{9,10},{10,1... | collective-permute-start | bytes 294920 | tf_op jit(solution)/shard_map/ppermute | solution.py:14
  22.9 1.4 fusion.71
  24.4 0.1 reshape.33
  24.5 0.7 reshape.34
  25.2 0.1 reshape.35
  25.3 1.1 copy.46
  26.4 0.0 collective-permute-done.3
  26.4 1.1 copy.49
  27.5 0.0 copy-start.10
  27.5 1.1 fusion.54
  28.7 0.0 copy-start.1
  28.7 0.3 fusion.50
  29.1 0.0 copy-start.5
  29.1 0.0 copy-start.12
  29.1 0.6 fusion.10
  29.7 0.2 copy-done.5
  30.0 0.4 fusion.31
  30.3 0.7 copy-done.11
  31.0 2.1 %convert_reduce_fusion = (f32[32]{0:T(128)S(1)}, bf16[32,64,128]{2,0,1:T(8,128)(2,1)S(1)}, bf16[32,64,128]{2,0,1:T(8,128)(2,1)}) fusion(bf16[32,64,128]{2,1,0:T(8,128)(2,1)S(1)} %copy-done.11, f32[64,128,32]{1,2,0:T(8,128)S(1)} %fusion.31, bf16[32,96,1]{1,0,2:T(8,128)(2,1)S(1)} %reshape.35, bf16[96,64,128]{2,0,1:T(8,128)(2,1)S(1)} %fusion.10), kind=kOutput, calls=%fused_computation.64 | convolution fusion | flops 56885216 | bytes 4200576 | tf_op jit(solution)/shard_map/ok,krq->orq/dot_general | solution.py:71
  33.1 0.6 fusion.38
  33.7 0.0 copy-start.6
  33.7 0.6 fusion.39
  34.4 0.1 reshape.31
  34.5 0.3 copy-done.2
  34.8 0.0 copy-done.6
  34.8 0.6 fusion.40
  35.4 0.1 reshape.30
  35.5 0.1 reshape.32
  35.6 1.3 collective-permute-start.5
  36.9 4.0 %collective-permute-start.4 = (bf16[32,16,128]{2,0,1:T(8,128)(2,1)S(1)}, bf16[32,16,128]{2,0,1:T(8,128)(2,1)S(1)}, u32[]{:S(2)}, u32[]{:S(2)}) collective-permute-start(bf16[32,16,128]{2,0,1:T(8,128)(2,1)S(1)} %get-tuple-element.40), channel_id=1, source_target_pairs={{0,16},{16,32},{32,48},{48,64},{64,80},{80,96},{96,112},{112,128},... | collective-permute-start | bytes 393224 | tf_op jit(solution)/shard_map/ppermute | solution.py:14
  41.0 1.1 collective-permute-done.5
  42.1 0.8 collective-permute-done.4
  42.9 0.1 pad_maximum_fusion.8
  43.0 0.3 fusion.67
  43.3 0.0 copy-start.3
  43.3 0.8 copy.56
  44.1 0.8 copy.58
  44.9 5.1 %collective-permute-start.7 = (bf16[32,96,16]{1,2,0:T(8,128)(2,1)S(1)}, bf16[32,96,16]{1,2,0:T(8,128)(2,1)S(1)}, u32[]{:S(2)}, u32[]{:S(2)}) collective-permute-start(bf16[32,96,16]{1,2,0:T(8,128)(2,1)S(1)} %copy.58), channel_id=1, source_target_pairs={{0,1},{1,2},{2,3},{3,4},{4,5},{5,6},{6,7},{7,8},{8,9},{9,10},{10,1... | collective-permute-start | bytes 294920 | tf_op jit(solution)/shard_map/ppermute | solution.py:14
  50.0 2.1 %collective-permute-start.6 = (bf16[32,96,16]{1,2,0:T(8,128)(2,1)S(1)}, bf16[32,96,16]{1,2,0:T(8,128)(2,1)S(1)}, u32[]{:S(2)}, u32[]{:S(2)}) collective-permute-start(bf16[32,96,16]{1,2,0:T(8,128)(2,1)S(1)} %copy.56), channel_id=1, source_target_pairs={{1,0},{2,1},{3,2},{4,3},{5,4},{6,5},{7,6},{8,7},{9,8},{10,9},{11,1... | collective-permute-start | bytes 294920 | tf_op jit(solution)/shard_map/ppermute | solution.py:14
  52.1 0.1 pad_maximum_fusion.11
  52.2 120.2 %all-reduce = (f32[3,3,32,32]{3,1,2,0:T(4,128)S(1)}, f32[32]{0:T(128)}) all-reduce(f32[3,3,32,32]{3,1,2,0:T(4,128)S(1)} %pad_maximum_fusion.11, f32[32]{0:T(128)S(1)} %broadcast_multiply_fusion), channel_id=1, replica_groups=mesh['row'=32,'col'=16] {'row','col'}, use_global_device_ids=true, to_apply=%region_0.0 | all-reduce | flops 9248 | bytes 73984 | tf_op jit(solution)/shard_map/psum | solution.py:87
  172.4 0.7 copy.65
  173.1 1.0 copy.63
  174.1 1.1 copy.57
  175.2 1.1 copy.59
  176.3 1.5 pad_maximum_fusion.7
  177.8 0.7 fusion.65
  178.5 0.0 copy-done.9
  178.5 0.4 fusion.16
  178.9 0.4 copy-done.8
  179.3 0.4 fusion.2
  179.7 0.4 copy-done.7
  180.0 0.4 fusion.35
  180.4 1.0 copy.64
  (24 shorter events, 0.2 us)
Async XLA Ops:
  0.6 7.8 %copy-start = (bf16[32,64,128]{2,1,0:T(8,128)(2,1)S(1)}, bf16[32,64,128]{2,1,0:T(8,128)(2,1)}, u32[]{:S(2)}) copy-start(bf16[32,64,128]{2,1,0:T(8,128)(2,1)} %param.4) | copy-start | bytes 1572868
  2.1 6.3 %collective-permute-start = (bf16[32,16,128]{2,0,1:T(8,128)(2,1)S(1)}, bf16[32,16,128]{2,0,1:T(8,128)(2,1)S(1)}, u32[]{:S(2)}, u32[]{:S(2)}) collective-permute-start(bf16[32,16,128]{2,0,1:T(8,128)(2,1)S(1)} %get-tuple-element.42), channel_id=1, source_target_pairs={{0,16},{16,32},{32,48},{48,64},{64,80},{80,96},{96,112},{112,128},... | collective-permute-start | bytes 393224 | tf_op jit(solution)/shard_map/ppermute | solution.py:14
  6.5 5.9 %collective-permute-start.1 = (bf16[32,16,128]{2,0,1:T(8,128)(2,1)S(1)}, bf16[32,16,128]{2,0,1:T(8,128)(2,1)S(1)}, u32[]{:S(2)}, u32[]{:S(2)}) collective-permute-start(bf16[32,16,128]{2,0,1:T(8,128)(2,1)S(1)} %get-tuple-element.41), channel_id=1, source_target_pairs={{16,0},{32,16},{48,32},{64,48},{80,64},{96,80},{112,96},{128,112},... | collective-permute-start | bytes 393224 | tf_op jit(solution)/shard_map/ppermute | solution.py:14
  8.4 4.3 %copy-start.4 = (bf16[32,16,128]{2,0,1:T(8,128)(2,1)}, bf16[32,16,128]{2,0,1:T(8,128)(2,1)S(1)}, u32[]{:S(2)}) copy-start(bf16[32,16,128]{2,0,1:T(8,128)(2,1)S(1)} %collective-permute-done) | copy-start | bytes 393220
  14.4 12.0 %collective-permute-start.3 = (bf16[32,96,16]{1,2,0:T(8,128)(2,1)S(1)}, bf16[32,96,16]{1,2,0:T(8,128)(2,1)S(1)}, u32[]{:S(2)}, u32[]{:S(2)}) collective-permute-start(bf16[32,96,16]{1,2,0:T(8,128)(2,1)S(1)} %copy.48), channel_id=1, source_target_pairs={{1,0},{2,1},{3,2},{4,3},{5,4},{6,5},{7,6},{8,7},{9,8},{10,9},{11,1... | collective-permute-start | bytes 294920 | tf_op jit(solution)/shard_map/ppermute | solution.py:14
  21.0 4.3 %collective-permute-start.2 = (bf16[32,96,16]{1,2,0:T(8,128)(2,1)S(1)}, bf16[32,96,16]{1,2,0:T(8,128)(2,1)S(1)}, u32[]{:S(2)}, u32[]{:S(2)}) collective-permute-start(bf16[32,96,16]{1,2,0:T(8,128)(2,1)S(1)} %copy.45), channel_id=1, source_target_pairs={{0,1},{1,2},{2,3},{3,4},{4,5},{5,6},{6,7},{7,8},{8,9},{9,10},{10,1... | collective-permute-start | bytes 294920 | tf_op jit(solution)/shard_map/ppermute | solution.py:14
  27.5 1.2 copy-start.10
  28.7 1.0 copy-start.1
  29.1 0.9 copy-start.5
  29.1 0.9 copy-start.12
  30.0 1.0 copy-start.11
  33.7 1.1 copy-start.2
  33.7 1.1 copy-start.6
  35.6 6.5 %collective-permute-start.5 = (bf16[32,16,128]{2,0,1:T(8,128)(2,1)S(1)}, bf16[32,16,128]{2,0,1:T(8,128)(2,1)S(1)}, u32[]{:S(2)}, u32[]{:S(2)}) collective-permute-start(bf16[32,16,128]{2,0,1:T(8,128)(2,1)S(1)} %get-tuple-element.39), channel_id=1, source_target_pairs={{16,0},{32,16},{48,32},{64,48},{80,64},{96,80},{112,96},{128,112},... | collective-permute-start | bytes 393224 | tf_op jit(solution)/shard_map/ppermute | solution.py:14
  36.9 5.9 %collective-permute-start.4 = (bf16[32,16,128]{2,0,1:T(8,128)(2,1)S(1)}, bf16[32,16,128]{2,0,1:T(8,128)(2,1)S(1)}, u32[]{:S(2)}, u32[]{:S(2)}) collective-permute-start(bf16[32,16,128]{2,0,1:T(8,128)(2,1)S(1)} %get-tuple-element.40), channel_id=1, source_target_pairs={{0,16},{16,32},{32,48},{48,64},{64,80},{80,96},{96,112},{112,128},... | collective-permute-start | bytes 393224 | tf_op jit(solution)/shard_map/ppermute | solution.py:14
  43.3 129.8 %copy-start.3 = (bf16[32,64,128]{2,0,1:T(8,128)(2,1)S(1)}, bf16[32,64,128]{2,0,1:T(8,128)(2,1)}, u32[]{:S(2)}) copy-start(bf16[32,64,128]{2,0,1:T(8,128)(2,1)} %get-tuple-element.30) | copy-start | bytes 1572868
  44.9 130.3 %collective-permute-start.7 = (bf16[32,96,16]{1,2,0:T(8,128)(2,1)S(1)}, bf16[32,96,16]{1,2,0:T(8,128)(2,1)S(1)}, u32[]{:S(2)}, u32[]{:S(2)}) collective-permute-start(bf16[32,96,16]{1,2,0:T(8,128)(2,1)S(1)} %copy.58), channel_id=1, source_target_pairs={{0,1},{1,2},{2,3},{3,4},{4,5},{5,6},{6,7},{7,8},{8,9},{9,10},{10,1... | collective-permute-start | bytes 294920 | tf_op jit(solution)/shard_map/ppermute | solution.py:14
  50.0 124.1 %collective-permute-start.6 = (bf16[32,96,16]{1,2,0:T(8,128)(2,1)S(1)}, bf16[32,96,16]{1,2,0:T(8,128)(2,1)S(1)}, u32[]{:S(2)}, u32[]{:S(2)}) collective-permute-start(bf16[32,96,16]{1,2,0:T(8,128)(2,1)S(1)} %copy.56), channel_id=1, source_target_pairs={{1,0},{2,1},{3,2},{4,3},{5,4},{6,5},{7,6},{8,7},{9,8},{10,9},{11,1... | collective-permute-start | bytes 294920 | tf_op jit(solution)/shard_map/ppermute | solution.py:14
  177.8 0.7 copy-start.9
  178.5 0.7 copy-start.8
  179.3 0.7 copy-start.7
where the time goes:
time: 182 us; the launch traced here: 181 us
  blocking collectives  120 us (66%)
  starting transfers between devices  26.7 us (15%)
  local copies, waits for them, and re-layouts  18.2 us (10%)
  waiting for transfers between devices  6.11 us (3%)
  matrix products  5.82 us (3%)
  other arithmetic  3.41 us (2%)
    psum x1, blocking collectives, shards(): lax.psum((local_weight, local_bias), ('row', 'col'))  120 us
    ppermute x8, starting transfers between devices, from_behind(): lax.ppermute(value, axis, [(source, source + steps) for source in range(i...  26.7 us
    unnamed x32, local copies, waits for them, and re-layouts  6.49 us
    ppermute x8, waiting for transfers between devices, from_behind(): lax.ppermute(value, axis, [(source, source + steps) for source in range(i...  6.11 us
    ppermute x4, local copies, waits for them, and re-layouts, from_behind(): lax.ppermute(value, axis, [(source, source + steps) for source in range(i...  4.41 us
  transfers between devices with their start and end apart: 8, of which 4 were waited for; matrix products, arithmetic and copies ran while one was open for 4% of the time, Pallas kernels for 0%

commit v1 on v0

--- a/solution.py
+++ b/solution.py
@@ -3,6 +3,8 @@
 import jax
 import jax.numpy as jnp
 from jax import lax
+from jax.experimental import pallas as pl
+from jax.experimental.pallas import tpu as pltpu
 from jax.sharding import PartitionSpec as P
 
 DILATION_PIXELS = 16
@@ -52,6 +54,109 @@
         ],
         axis=0,
     )
+
+
+MESH = pl.DeviceIdType.MESH
+PLANE = 32
+DEPTH = 16
+
+
+def coordinates():
+    row = lax.axis_index("row")
+    col = lax.axis_index("col")
+    z = row % DEPTH
+    y = (col // 8) * 2 + row // DEPTH
+    x = (col // 2) % 4
+    core = col % 2
+    return row, col, z, y, x, core
+
+
+def plane_member(y, x, core, z):
+    col = (y // 2) * 8 + x * 2 + core
+    row = (y % 2) * DEPTH + z
+    return {"row": row, "col": col}, (y % 2) * 16 + col
+
+
+def plane_offsets():
+    far = (2, 1, 3, 0)
+    offsets = [(dy, dx, dc) for dy in far for dx in far for dc in (1, 0)]
+    offsets = [offset for offset in offsets if offset != (0, 0, 0)]
+    hops = lambda d: min(d, 4 - d)
+    return sorted(offsets, key=lambda o: -(hops(o[0]) + hops(o[1])))
+
+
+def plane_peers():
+    row, col, z, y, x, core = coordinates()
+    peers = []
+    for dy, dx, dc in plane_offsets():
+        peers.append(plane_member((y + dy) % 4, (x + dx) % 4, (core + dc) % 2, z))
+    return peers
+
+
+def depth_peers():
+    row, col, z, y, x, core = coordinates()
+    order = sorted(range(1, DEPTH), key=lambda k: -min(k, DEPTH - k))
+    return [{"row": (row // DEPTH) * DEPTH + (z + k) % DEPTH, "col": col} for k in order]
+
+
+def reduce_kernel(terms, total, gathered, layers, piece, send_sem, recv_sem):
+    row, col, z, y, x, core = coordinates()
+    me = (row // DEPTH) * 16 + col
+    plane = plane_peers()
+    column = depth_peers()
+    barrier = pltpu.get_barrier_semaphore()
+    for peer in [p for p, _ in plane] + column:
+        pl.semaphore_signal(barrier, inc=1, device_id=peer, device_id_type=MESH)
+    pl.semaphore_wait(barrier, len(plane) + len(column))
+
+    def finish(k, buffer):
+        copy = pltpu.make_async_copy(buffer, buffer, recv_sem.at[k])
+        copy.wait()
+
+    def sent(k, buffer):
+        pltpu.make_async_copy(buffer, buffer, send_sem.at[k]).wait()
+
+    for peer, index in plane:
+        pltpu.make_async_remote_copy(
+            terms.at[index], gathered.at[me], send_sem.at[0], recv_sem.at[0], device_id=peer, device_id_type=MESH
+        ).start()
+    gathered[me] = terms[me]
+    finish(0, gathered.at[pl.ds(0, PLANE - 1)])
+    piece[0] = jnp.sum(gathered[...], axis=0)
+    for peer in column:
+        pltpu.make_async_remote_copy(
+            piece.at[0], layers.at[z], send_sem.at[1], recv_sem.at[1], device_id=peer, device_id_type=MESH
+        ).start()
+    layers[z] = piece[0]
+    finish(1, layers.at[pl.ds(0, DEPTH - 1)])
+    piece[1] = jnp.sum(layers[...], axis=0)
+    for peer, index in plane:
+        pltpu.make_async_remote_copy(
+            piece.at[1], total.at[me], send_sem.at[2], recv_sem.at[2], device_id=peer, device_id_type=MESH
+        ).start()
+    total[me] = piece[1]
+    finish(2, total.at[pl.ds(0, PLANE - 1)])
+    sent(0, gathered.at[pl.ds(0, PLANE - 1)])
+    sent(1, layers.at[pl.ds(0, DEPTH - 1)])
+    sent(2, total.at[pl.ds(0, PLANE - 1)])
+
+
+def reduce_all(terms):
+    shape = terms.shape
+    return pl.pallas_call(
+        reduce_kernel,
+        out_shape=jax.ShapeDtypeStruct(shape, jnp.float32),
+        in_specs=[pl.BlockSpec(memory_space=pltpu.VMEM)],
+        out_specs=pl.BlockSpec(memory_space=pltpu.VMEM),
+        scratch_shapes=[
+            pltpu.VMEM(shape, jnp.float32),
+            pltpu.VMEM((DEPTH,) + shape[1:], jnp.float32),
+            pltpu.VMEM((2,) + shape[1:], jnp.float32),
+            pltpu.SemaphoreType.DMA((3,)),
+            pltpu.SemaphoreType.DMA((3,)),
+        ],
+        compiler_params=pltpu.CompilerParams(collective_id=0, has_side_effects=True),
+    )(terms)
 
 
 def shards(image, weight, bias, cotangent):
@@ -81,10 +186,17 @@
             jnp.einsum("orq,krq->ok", preact_gradient, stacked, preferred_element_type=jnp.float32)
             * scale
         )
-        taps.append(jnp.transpose(joined.reshape(channels, 3, channels), (1, 0, 2)))
-    local_weight = jnp.stack(taps)
+        taps.append(joined)
     local_bias = jnp.sum(preact_gradient.astype(jnp.float32), axis=(1, 2)) * scale
-    grad_weight, grad_bias = lax.psum((local_weight, local_bias), ("row", "col"))
+    taps[0] = jnp.concatenate([taps[0], local_bias[:, None]], axis=1)
+    padded = [jnp.pad(tap, ((0, 0), (0, 128 - tap.shape[1]))) for tap in taps]
+    terms = jnp.concatenate(padded, axis=1)[:, None, :]
+    total_terms = reduce_all(terms)[:, 0, :]
+    grad_bias = total_terms[:, 3 * channels]
+    grad_weight = jnp.transpose(
+        total_terms.reshape(channels, 3, 128)[:, :, : 3 * channels].reshape(channels, 3, 3, channels),
+        (1, 2, 0, 3),
+    )
     grad_ext = extended(preact_gradient)
     total = jnp.zeros(image.shape, jnp.float32)
     for row_offset in (-1, 0, 1):

time: 182 us -> 106 us (0.58)
  the two profiles are of different devices: /device:TPU:1 before, /device:TPU:7 now
where the time goes in v1:
time: 106 us; the launch traced here: 105 us
  Pallas kernels  34.8 us (33%)
  starting transfers between devices  27.7 us (26%)
  local copies, waits for them, and re-layouts  20 us (19%)
  waiting for transfers between devices  11.9 us (11%)
  matrix products  5.07 us (5%)
  other arithmetic  4.38 us (4%)
    pallas_call x1, Pallas kernels, reduce_all(): pl.pallas_call(reduce_kernel, out_shape=jax.ShapeDtypeStruct(shape, jnp.f...  34.8 us
    ppermute x8, starting transfers between devices, from_behind(): lax.ppermute(value, axis, [(source, source + steps) for source in range(i...  27.7 us
    ppermute x8, waiting for transfers between devices, from_behind(): lax.ppermute(value, axis, [(source, source + steps) for source in range(i...  11.9 us
    unnamed x31, local copies, waits for them, and re-layouts  7 us
    ppermute x4, local copies, waits for them, and re-layouts, from_behind(): lax.ppermute(value, axis, [(source, source + steps) for source in range(i...  4.41 us
    concatenate x2, other arithmetic, extended(): return jnp.concatenate([left_margin, tall_block, right_margin], axis=2)  2.62 us
  transfers between devices with their start and end apart: 8, of which 3 were waited for; matrix products, arithmetic and copies ran while one was open for 10% of the time, Pallas kernels for 33%

profile of v1, /device:TPU:7, one launch (start us, length us, event | category | flops | bytes accessed | tf_op | source)
XLA Modules:
  0.0 105.0 jit_solution(12125741041073344009)
XLA Ops:
  0.6 1.4 %copy.42 = bf16[32,64,128]{2,0,1:T(8,128)(2,1)S(1)} copy(bf16[32,64,128]{2,1,0:T(8,128)(2,1)} %param.4) | data formatting | bytes 1048576 | tf_op args[0]
  2.1 3.5 %collective-permute-start = (bf16[32,16,128]{2,0,1:T(8,128)(2,1)S(1)}, bf16[32,16,128]{2,0,1:T(8,128)(2,1)S(1)}, u32[]{:S(2)}, u32[]{:S(2)}) collective-permute-start(bf16[32,16,128]{2,0,1:T(8,128)(2,1)S(1)} %get-tuple-element.40), channel_id=1, source_target_pairs={{0,16},{16,32},{32,48},{48,64},{64,80},{80,96},{96,112},{112,128},... | collective-permute-start | bytes 393224 | tf_op jit(solution)/shard_map/ppermute | solution.py:16
  5.7 1.3 %collective-permute-start.1 = (bf16[32,16,128]{2,0,1:T(8,128)(2,1)S(1)}, bf16[32,16,128]{2,0,1:T(8,128)(2,1)S(1)}, u32[]{:S(2)}, u32[]{:S(2)}) collective-permute-start(bf16[32,16,128]{2,0,1:T(8,128)(2,1)S(1)} %get-tuple-element.39), channel_id=1, source_target_pairs={{16,0},{32,16},{48,32},{64,48},{80,64},{96,80},{112,96},{128,112},... | collective-permute-start | bytes 393224 | tf_op jit(solution)/shard_map/ppermute | solution.py:16
  7.0 0.9 collective-permute-done
  7.9 0.4 constant_dynamic-update-slice_fusion.1
  8.2 3.8 %collective-permute-done.1 = bf16[32,16,128]{2,0,1:T(8,128)(2,1)S(1)} collective-permute-done((bf16[32,16,128]{2,0,1:T(8,128)(2,1)S(1)}, bf16[32,16,128]{2,0,1:T(8,128)(2,1)S(1)}, u32[]{:S(2)}, u32[]{:S(2)}) %collective-permute-start.1) | collective-permute-done | bytes 131104 | tf_op jit(solution)/shard_map/ppermute | solution.py:16
  12.0 0.3 fusion.69
  12.4 0.8 copy.45
  13.2 0.8 copy.48
  14.0 3.5 %collective-permute-start.3 = (bf16[32,96,16]{1,2,0:T(8,128)(2,1)S(1)}, bf16[32,96,16]{1,2,0:T(8,128)(2,1)S(1)}, u32[]{:S(2)}, u32[]{:S(2)}) collective-permute-start(bf16[32,96,16]{1,2,0:T(8,128)(2,1)S(1)} %copy.48), channel_id=1, source_target_pairs={{1,0},{2,1},{3,2},{4,3},{5,4},{6,5},{7,6},{8,7},{9,8},{10,9},{11,1... | collective-permute-start | bytes 294920 | tf_op jit(solution)/shard_map/ppermute | solution.py:16
  17.6 5.6 %collective-permute-start.2 = (bf16[32,96,16]{1,2,0:T(8,128)(2,1)S(1)}, bf16[32,96,16]{1,2,0:T(8,128)(2,1)S(1)}, u32[]{:S(2)}, u32[]{:S(2)}) collective-permute-start(bf16[32,96,16]{1,2,0:T(8,128)(2,1)S(1)} %copy.45), channel_id=1, source_target_pairs={{0,1},{1,2},{2,3},{3,4},{4,5},{5,6},{6,7},{7,8},{8,9},{9,10},{10,1... | collective-permute-start | bytes 294920 | tf_op jit(solution)/shard_map/ppermute | solution.py:16
  23.2 1.4 %fusion.72 = (bf16[1,3,32,32]{3,2,1,0:T(8,128)(2,1)}, bf16[32,3,32]{2,0,1:T(8,128)(2,1)S(1)}, bf16[32,3,32]{2,0,1:T(8,128)(2,1)S(1)}, bf16[32,3,32]{2,0,1:T(8,12...) fusion(bf16[3,3,32,32]{3,2,1,0:T(8,128)(2,1)} %param.5), kind=kLoop, calls=%fused_computation.102 | loop fusion | bytes 55296 | tf_op jit(solution)/shard_map/slice | solution.py:172
  24.6 0.1 reshape.34
  24.8 0.7 reshape.35
  25.5 0.1 reshape.36
  25.6 0.0 collective-permute-done.2
  25.6 1.1 %copy.46 = bf16[32,96,16]{2,0,1:T(8,128)(2,1)S(1)} copy(bf16[32,96,16]{1,2,0:T(8,128)(2,1)S(1)} %collective-permute-done.2) | data formatting | bytes 196608 | tf_op jit(solution)/shard_map/ppermute | solution.py:16
  26.7 0.0 collective-permute-done.3
  26.7 1.1 %copy.49 = bf16[32,96,16]{2,0,1:T(8,128)(2,1)S(1)} copy(bf16[32,96,16]{1,2,0:T(8,128)(2,1)S(1)} %collective-permute-done.3) | data formatting | bytes 196608 | tf_op jit(solution)/shard_map/ppermute | solution.py:16
  27.8 0.0 copy-start.9
  27.8 1.1 %fusion.54 = (bf16[32,64,128]{2,0,1:T(8,128)(2,1)S(1)}, bf16[32,64,128]{2,0,1:T(8,128)(2,1)S(1)}, bf16[32,64,128]{2,0,1:T(8,128)(2,1)S(1)}, bf16[32,64,128]{2,0,1:T(8,128)(2,1)S(1)}) fusion(bf16[32,96,16]{2,0,1:T(8,128)(2,1)S(1)} %copy.46, bf16[32,96,128]{2,0,1:T(8,128)(2,1)S(1)} %constant_dynamic-update-slice_fusion, bf16[32,96,16]{2,0,1:T(8,128)(2,1)S(1)} %copy.49), kind=kLoop, calls=%fused_computation.71 | loop fusion | flops 4194304 | bytes 3080192 | tf_op jit(solution)/shard_map/concatenate | solution.py:38
  28.9 0.0 copy-start.1
  29.0 0.3 fusion.50
  29.3 0.0 copy-start.4
  29.3 0.0 copy-start.11
  29.3 0.6 fusion.10
  30.0 0.2 copy-done.4
  30.2 0.4 fusion.31
  30.6 0.7 copy-done.10
  31.3 1.3 %convert_reduce_fusion = (f32[32]{0:T(128)S(1)}, bf16[32,64,128]{2,0,1:T(8,128)(2,1)S(1)}, bf16[32,64,128]{2,0,1:T(8,128)(2,1)S(1)}) fusion(bf16[32,64,128]{2,1,0:T(8,128)(2,1)S(1)} %copy-done.10, f32[64,128,32]{1,2,0:T(8,128)S(1)} %fusion.31, bf16[32,96,1]{1,0,2:T(8,128)(2,1)S(1)} %reshape.36, bf16[96,64,128]{2,0,1:T(8,128)(2,1)S(1)} %fusion.10), kind=kOutput, calls=%fused_computation.64 | convolution fusion | flops 56885216 | bytes 4200576 | tf_op jit(solution)/shard_map/ok,krq->orq/dot_general | solution.py:176
  32.6 0.6 fusion.38
  33.2 0.0 copy-start.5
  33.3 0.6 fusion.39
  33.9 0.1 copy.63
  34.0 1.3 %collective-permute-start.5 = (bf16[32,16,128]{2,0,1:T(8,128)(2,1)S(1)}, bf16[32,16,128]{2,0,1:T(8,128)(2,1)S(1)}, u32[]{:S(2)}, u32[]{:S(2)}) collective-permute-start(bf16[32,16,128]{2,0,1:T(8,128)(2,1)S(1)} %get-tuple-element.37), channel_id=1, source_target_pairs={{16,0},{32,16},{48,32},{64,48},{80,64},{96,80},{112,96},{128,112},... | collective-permute-start | bytes 393224 | tf_op jit(solution)/shard_map/ppermute | solution.py:16
  35.3 4.4 %collective-permute-start.4 = (bf16[32,16,128]{2,0,1:T(8,128)(2,1)S(1)}, bf16[32,16,128]{2,0,1:T(8,128)(2,1)S(1)}, u32[]{:S(2)}, u32[]{:S(2)}) collective-permute-start(bf16[32,16,128]{2,0,1:T(8,128)(2,1)S(1)} %get-tuple-element.38), channel_id=1, source_target_pairs={{0,16},{16,32},{32,48},{48,64},{64,80},{80,96},{96,112},{112,128},... | collective-permute-start | bytes 393224 | tf_op jit(solution)/shard_map/ppermute | solution.py:16
  39.7 0.6 fusion.40
  40.3 0.1 select_maximum_fusion.2
  40.4 0.7 broadcast_in_dim.2.terms
  41.1 34.8 %shard_map.75 = f32[32,1,384]{2,1,0:T(1,128)} custom-call(f32[32,1,384]{2,1,0:T(1,128)} %broadcast_in_dim.2.terms), custom_call_target="tpu_custom_call" | custom-call | tf_op jit(solution)/shard_map/pallas_call | solution.py:146
  75.9 0.8 copy.76
  76.8 0.9 reduce
  77.7 0.1 reshape.33
  77.8 0.7 copy.67
  78.5 1.0 copy.65
  79.5 0.1 pad_maximum_fusion.8
  79.6 0.3 fusion.68
  79.9 0.8 copy.56
  80.8 0.8 copy.58
  81.6 6.2 %collective-permute-start.7 = (bf16[32,96,16]{1,2,0:T(8,128)(2,1)S(1)}, bf16[32,96,16]{1,2,0:T(8,128)(2,1)S(1)}, u32[]{:S(2)}, u32[]{:S(2)}) collective-permute-start(bf16[32,96,16]{1,2,0:T(8,128)(2,1)S(1)} %copy.58), channel_id=1, source_target_pairs={{0,1},{1,2},{2,3},{3,4},{4,5},{5,6},{6,7},{7,8},{8,9},{9,10},{10,1... | collective-permute-start | bytes 294920 | tf_op jit(solution)/shard_map/ppermute | solution.py:16
  87.7 1.9 %collective-permute-start.6 = (bf16[32,96,16]{1,2,0:T(8,128)(2,1)S(1)}, bf16[32,96,16]{1,2,0:T(8,128)(2,1)S(1)}, u32[]{:S(2)}, u32[]{:S(2)}) collective-permute-start(bf16[32,96,16]{1,2,0:T(8,128)(2,1)S(1)} %copy.56), channel_id=1, source_target_pairs={{1,0},{2,1},{3,2},{4,3},{5,4},{6,5},{7,6},{8,7},{9,8},{10,9},{11,1... | collective-permute-start | bytes 294920 | tf_op jit(solution)/shard_map/ppermute | solution.py:16
  89.7 0.7 slice_reduce_fusion
  90.4 7.3 %collective-permute-done.6 = bf16[32,96,16]{1,2,0:T(8,128)(2,1)S(1)} collective-permute-done((bf16[32,96,16]{1,2,0:T(8,128)(2,1)S(1)}, bf16[32,96,16]{1,2,0:T(8,128)(2,1)S(1)}, u32[]{:S(2)}, u32[]{:S(2)}) %collective-permute-start.6) | collective-permute-done | bytes 98336 | tf_op jit(solution)/shard_map/ppermute | solution.py:16
  97.6 1.1 %copy.57 = bf16[32,96,16]{2,0,1:T(8,128)(2,1)S(1)} copy(bf16[32,96,16]{1,2,0:T(8,128)(2,1)S(1)} %collective-permute-done.6) | data formatting | bytes 196608 | tf_op jit(solution)/shard_map/ppermute | solution.py:16
  98.8 1.1 %copy.59 = bf16[32,96,16]{2,0,1:T(8,128)(2,1)S(1)} copy(bf16[32,96,16]{1,2,0:T(8,128)(2,1)S(1)} %collective-permute-done.7) | data formatting | bytes 196608 | tf_op jit(solution)/shard_map/ppermute | solution.py:16
  99.9 1.5 %pad_maximum_fusion.7 = (bf16[32,96,144]{2,0,1:T(8,128)(2,1)S(1)}, bf16[32,96,144]{2,0,1:T(8,128)(2,1)S(1)}) fusion(bf16[32,96,16]{2,0,1:T(8,128)(2,1)S(1)} %copy.57, bf16[32,16,128]{2,0,1:T(8,128)(2,1)S(1)} %collective-permute-done.5, bf16[32,64,128]{2,0,1:T(8,128)(2,1)S(1)} %get-tuple-element.17, bf16[32,16,128]{2,0,1:T(8,128)(2,1)S(1)} %collective-permute-done.4, ...), kind=kLoop, calls=%fused_computation.27 | loop fusion | flops 7077888 | bytes 2752512 | tf_op jit(solution)/shard_map/concatenate | solution.py:38
  101.4 0.7 fusion.66
  102.1 0.0 copy-done.8
  102.1 0.4 fusion.16
  102.5 0.4 copy-done.7
  102.8 0.4 fusion.2
  103.2 0.4 copy-done.6
  103.6 0.4 fusion.35
  104.0 1.0 copy.66
  (28 shorter events, 0.2 us)
Async XLA Ops:
  0.6 7.2 %copy-start = (bf16[32,64,128]{2,1,0:T(8,128)(2,1)S(1)}, bf16[32,64,128]{2,1,0:T(8,128)(2,1)}, u32[]{:S(2)}) copy-start(bf16[32,64,128]{2,1,0:T(8,128)(2,1)} %param.4) | copy-start | bytes 1572868
  2.1 5.7 %collective-permute-start = (bf16[32,16,128]{2,0,1:T(8,128)(2,1)S(1)}, bf16[32,16,128]{2,0,1:T(8,128)(2,1)S(1)}, u32[]{:S(2)}, u32[]{:S(2)}) collective-permute-start(bf16[32,16,128]{2,0,1:T(8,128)(2,1)S(1)} %get-tuple-element.40), channel_id=1, source_target_pairs={{0,16},{16,32},{32,48},{48,64},{64,80},{80,96},{96,112},{112,128},... | collective-permute-start | bytes 393224 | tf_op jit(solution)/shard_map/ppermute | solution.py:16
  5.7 6.4 %collective-permute-start.1 = (bf16[32,16,128]{2,0,1:T(8,128)(2,1)S(1)}, bf16[32,16,128]{2,0,1:T(8,128)(2,1)S(1)}, u32[]{:S(2)}, u32[]{:S(2)}) collective-permute-start(bf16[32,16,128]{2,0,1:T(8,128)(2,1)S(1)} %get-tuple-element.39), channel_id=1, source_target_pairs={{16,0},{32,16},{48,32},{64,48},{80,64},{96,80},{112,96},{128,112},... | collective-permute-start | bytes 393224 | tf_op jit(solution)/shard_map/ppermute | solution.py:16
  7.8 4.5 %copy-start.3 = (bf16[32,16,128]{2,0,1:T(8,128)(2,1)}, bf16[32,16,128]{2,0,1:T(8,128)(2,1)S(1)}, u32[]{:S(2)}) copy-start(bf16[32,16,128]{2,0,1:T(8,128)(2,1)S(1)} %collective-permute-done) | copy-start | bytes 393220
  14.0 12.7 %collective-permute-start.3 = (bf16[32,96,16]{1,2,0:T(8,128)(2,1)S(1)}, bf16[32,96,16]{1,2,0:T(8,128)(2,1)S(1)}, u32[]{:S(2)}, u32[]{:S(2)}) collective-permute-start(bf16[32,96,16]{1,2,0:T(8,128)(2,1)S(1)} %copy.48), channel_id=1, source_target_pairs={{1,0},{2,1},{3,2},{4,3},{5,4},{6,5},{7,6},{8,7},{9,8},{10,9},{11,1... | collective-permute-start | bytes 294920 | tf_op jit(solution)/shard_map/ppermute | solution.py:16
  17.6 8.0 %collective-permute-start.2 = (bf16[32,96,16]{1,2,0:T(8,128)(2,1)S(1)}, bf16[32,96,16]{1,2,0:T(8,128)(2,1)S(1)}, u32[]{:S(2)}, u32[]{:S(2)}) collective-permute-start(bf16[32,96,16]{1,2,0:T(8,128)(2,1)S(1)} %copy.45), channel_id=1, source_target_pairs={{0,1},{1,2},{2,3},{3,4},{4,5},{5,6},{6,7},{7,8},{8,9},{9,10},{10,1... | collective-permute-start | bytes 294920 | tf_op jit(solution)/shard_map/ppermute | solution.py:16
  27.8 1.2 %copy-start.9 = (bf16[32,96,1]{1,0,2:T(8,128)(2,1)S(1)}, bf16[32,96,1]{1,0,2:T(8,128)(2,1)}, u32[]{:S(2)}) copy-start(bf16[32,96,1]{1,0,2:T(8,128)(2,1)} %reshape.35) | copy-start | bytes 18436
  28.9 1.0 copy-start.1
  29.3 0.9 copy-start.4
  29.3 0.9 copy-start.11
  30.2 1.0 copy-start.10
  33.2 6.5 %copy-start.2 = (bf16[32,64,128]{2,0,1:T(8,128)(2,1)S(1)}, bf16[32,64,128]{2,0,1:T(8,128)(2,1)}, u32[]{:S(2)}) copy-start(bf16[32,64,128]{2,0,1:T(8,128)(2,1)} %copy-done.1) | copy-start | bytes 1572868
  33.2 6.5 %copy-start.5 = (bf16[32,16,128]{2,0,1:T(8,128)(2,1)S(1)}, bf16[32,16,128]{2,0,1:T(8,128)(2,1)}, u32[]{:S(2)}) copy-start(bf16[32,16,128]{2,0,1:T(8,128)(2,1)} %copy-done.3) | copy-start | bytes 393220
  34.0 45.5 %collective-permute-start.5 = (bf16[32,16,128]{2,0,1:T(8,128)(2,1)S(1)}, bf16[32,16,128]{2,0,1:T(8,128)(2,1)S(1)}, u32[]{:S(2)}, u32[]{:S(2)}) collective-permute-start(bf16[32,16,128]{2,0,1:T(8,128)(2,1)S(1)} %get-tuple-element.37), channel_id=1, source_target_pairs={{16,0},{32,16},{48,32},{64,48},{80,64},{96,80},{112,96},{128,112},... | collective-permute-start | bytes 393224 | tf_op jit(solution)/shard_map/ppermute | solution.py:16
  35.3 44.2 %collective-permute-start.4 = (bf16[32,16,128]{2,0,1:T(8,128)(2,1)S(1)}, bf16[32,16,128]{2,0,1:T(8,128)(2,1)S(1)}, u32[]{:S(2)}, u32[]{:S(2)}) collective-permute-start(bf16[32,16,128]{2,0,1:T(8,128)(2,1)S(1)} %get-tuple-element.38), channel_id=1, source_target_pairs={{0,16},{16,32},{32,48},{48,64},{64,80},{80,96},{96,112},{112,128},... | collective-permute-start | bytes 393224 | tf_op jit(solution)/shard_map/ppermute | solution.py:16
  81.6 17.2 %collective-permute-start.7 = (bf16[32,96,16]{1,2,0:T(8,128)(2,1)S(1)}, bf16[32,96,16]{1,2,0:T(8,128)(2,1)S(1)}, u32[]{:S(2)}, u32[]{:S(2)}) collective-permute-start(bf16[32,96,16]{1,2,0:T(8,128)(2,1)S(1)} %copy.58), channel_id=1, source_target_pairs={{0,1},{1,2},{2,3},{3,4},{4,5},{5,6},{6,7},{7,8},{8,9},{9,10},{10,1... | collective-permute-start | bytes 294920 | tf_op jit(solution)/shard_map/ppermute | solution.py:16
  87.7 9.9 %collective-permute-start.6 = (bf16[32,96,16]{1,2,0:T(8,128)(2,1)S(1)}, bf16[32,96,16]{1,2,0:T(8,128)(2,1)S(1)}, u32[]{:S(2)}, u32[]{:S(2)}) collective-permute-start(bf16[32,96,16]{1,2,0:T(8,128)(2,1)S(1)} %copy.56), channel_id=1, source_target_pairs={{1,0},{2,1},{3,2},{4,3},{5,4},{6,5},{7,6},{8,7},{9,8},{10,9},{11,1... | collective-permute-start | bytes 294920 | tf_op jit(solution)/shard_map/ppermute | solution.py:16
  101.4 0.7 copy-start.8
  102.1 0.7 copy-start.7
  102.8 0.7 copy-start.6

commit v2 on v0

v2 whole, which is shorter than its diff:
```python
import math

import jax
import jax.numpy as jnp
from jax import lax
from jax.experimental import pallas as pl
from jax.experimental.pallas import tpu as pltpu
from jax.sharding import PartitionSpec as P

MESH = pl.DeviceIdType.MESH
BF16 = jnp.bfloat16
F32 = jnp.float32
DIL = 16
LANES = 128
PLANE = 32
DEPTH = 16
COEF = 0.7978845608
CUBIC = 0.044715


def ring_order(count):
    return sorted(range(1, count), key=lambda k: -min(k, count - k))


def gelu_pair(z):
    square = z * z
    t = jnp.tanh(z * (COEF + (COEF * CUBIC) * square))
    half = 0.5 + 0.5 * t
    bend = (1.0 - t * t) * (0.5 * COEF + (1.5 * COEF * CUBIC) * square)
    return z * half, half + z * bend


def lanes_of(row, count=1):
    return slice(row * LANES, (row + count) * LANES)


def body(
    rows, scale,
    image, weight, bias, cotangent,
    act_out, grad_out, gw_out, gb_out,
    xin, cin, cot, stack, gstack, xleft, xright, gleft, gright,
    pack_l, pack_r, act, act_c, grad_c, accs,
    terms, gathered, layers, piece, total,
    local_sem, xsend, xrecv, gsend, grecv, rsend, rrecv, chain_a, chain_b,
):
    channels = image.shape[0]
    ext = rows + 2 * DIL
    groups = rows // 8
    row = lax.axis_index("row")
    col = lax.axis_index("col")
    nrow, ncol = lax.axis_size("row"), lax.axis_size("col")
    z = row % DEPTH
    y = (col // 8) * 2 + row // DEPTH
    x = (col // 2) % 4
    core = col % 2
    me = (row // DEPTH) * 16 + col

    def at(drow, dcol):
        return {"row": (row + drow + nrow) % nrow, "col": (col + dcol + ncol) % ncol}

    def deep(k):
        return {"row": (row // DEPTH) * DEPTH + (z + k + DEPTH) % DEPTH, "col": col}

    hops = lambda d: min(d, 4 - d)
    offsets = [(dy, dx, dc) for dy in range(4) for dx in range(4) for dc in range(2)][1:]
    offsets = sorted(offsets, key=lambda o: -(hops(o[0]) + hops(o[1])))
    plane = []
    for dy, dx, dc in offsets:
        py, px, pc = (y + dy) % 4, (x + dx) % 4, (core + dc) % 2
        pcol = (py // 2) * 8 + px * 2 + pc
        plane.append(({"row": (py % 2) * DEPTH + z, "col": pcol}, (py % 2) * 16 + pcol))

    barrier = pltpu.get_barrier_semaphore()
    near = [at(-1, 0), at(1, 0), at(-1, -1), at(-1, 1), at(1, -1), at(1, 1)]
    near += [deep(k) for k in (3, -3, 2, -2, 1, -1)]
    greeted = near + [peer for peer, _ in plane]
    for peer in greeted:
        pl.semaphore_signal(barrier, inc=1, device_id=peer, device_id_type=MESH)

    load_x = pltpu.make_async_copy(image, xin.at[:, DIL : DIL + rows, :], local_sem.at[0])
    load_c = pltpu.make_async_copy(cotangent, cin, local_sem.at[1])
    load_x.start()
    load_c.start()

    lane = lax.broadcasted_iota(jnp.int32, (channels, LANES), 1)
    slot = lane // DIL
    forward = [
        jnp.concatenate([weight[a, e] for e in range(3)], axis=1) for a in range(3)
    ]
    backward = [
        jnp.concatenate([weight[2 - a, 2 - e].T for e in range(3)], axis=1) for a in range(3)
    ]
    sub = lax.broadcasted_iota(jnp.int32, (channels, channels), 0)
    lan = lax.broadcasted_iota(jnp.int32, (channels, channels), 1)
    offset = jnp.sum(jnp.where(sub == lan, bias[...], 0.0), axis=1, keepdims=True)
    accs[...] = jnp.zeros_like(accs)

    top, bottom = row == 0, row == nrow - 1
    first, last = col == 0, col == ncol - 1
    has = {
        "u": row > 0, "d": row < nrow - 1, "l": col > 0, "r": col < ncol - 1,
        "ul": (row > 0) & (col > 0), "ur": (row > 0) & (col < ncol - 1),
        "dl": (row < nrow - 1) & (col > 0), "dr": (row < nrow - 1) & (col < ncol - 1),
    }
    step = {
        "u": (-1, 0), "d": (1, 0), "l": (0, -1), "r": (0, 1),
        "ul": (-1, -1), "ur": (-1, 1), "dl": (1, -1), "dr": (1, 1),
    }
    mirror = {"u": "d", "d": "u", "l": "r", "r": "l", "ul": "dr", "dr": "ul", "ur": "dl", "dl": "ur"}
    names = list(step)

    def halo_copies(top_src, bottom_src, top_dst, bottom_dst, left, right, send, recv):
        src_dst = {
            "u": (top_src, bottom_dst),
            "d": (bottom_src, top_dst),
            "l": (pack_l, right.at[2 : 2 + groups]),
            "r": (pack_r, left.at[2 : 2 + groups]),
            "ul": (pack_l.at[0:2], right.at[2 + groups : 4 + groups]),
            "ur": (pack_r.at[0:2], left.at[2 + groups : 4 + groups]),
            "dl": (pack_l.at[groups - 2 : groups], right.at[0:2]),
            "dr": (pack_r.at[groups - 2 : groups], left.at[0:2]),
        }
        return {
            n: pltpu.make_async_remote_copy(
                src, dst, send.at[names.index(n)], recv.at[names.index(n)],
                device_id=at(*step[n]), device_id_type=MESH,
            )
            for n, (src, dst) in src_dst.items()
        }

    def when_each(directions, predicate, action):
        for n in directions:
            pl.when(predicate(n))(lambda n=n: action(n))

    def send(copies, directions):
        when_each(directions, lambda n: has[n], lambda n: copies[n].start())

    def await_from(copies, directions):
        when_each(directions, lambda n: has[n], lambda n: copies[mirror[n]].wait_recv())

    def await_sent(copies):
        when_each(names, lambda n: has[n], lambda n: copies[n].wait_send())

    def zero_edges(left, right, top_dst, bottom_dst):
        pl.when(first)(lambda: left.__setitem__(Ellipsis, jnp.zeros_like(left)))
        pl.when(last)(lambda: right.__setitem__(Ellipsis, jnp.zeros_like(right)))

        @pl.when(top)
        def _():
            top_dst[...] = jnp.zeros(top_dst.shape, BF16)
            left[0:2] = jnp.zeros((2,) + left.shape[1:], BF16)
            right[0:2] = jnp.zeros((2,) + left.shape[1:], BF16)

        @pl.when(bottom)
        def _():
            bottom_dst[...] = jnp.zeros(bottom_dst.shape, BF16)
            left[2 + groups : 4 + groups] = jnp.zeros((2,) + left.shape[1:], BF16)
            right[2 + groups : 4 + groups] = jnp.zeros((2,) + left.shape[1:], BF16)

    def pack(source, g):
        lefts, rights = None, None
        for k in range(8):
            v = source[channels : 2 * channels, lanes_of(DIL + 8 * g + k)]
            a = v if k == 0 else pltpu.roll(v, DIL * k, 1)
            b = v if k == 7 else pltpu.roll(v, DIL * k + DIL, 1)
            lefts = a if k == 0 else jnp.where(slot == k, a, lefts)
            rights = b if k == 0 else jnp.where(slot == k, b, rights)
        pack_l[g] = lefts
        pack_r[g] = rights

    def shift_row(source, r):
        v = source[channels : 2 * channels, lanes_of(r)]
        source[0:channels, lanes_of(r)] = pltpu.roll(v, DIL, 1)
        source[2 * channels : 3 * channels, lanes_of(r)] = pltpu.roll(v, LANES - DIL, 1)

    def merge_group(source, left, right, g):
        lv, rv = left[g], right[g]
        for k in range(8):
            r = lanes_of(8 * g + k)
            a = lv if k == 0 else pltpu.roll(lv, LANES - DIL * k, 1)
            b = rv if k == 7 else pltpu.roll(rv, LANES - DIL - DIL * k, 1)
            source[0:channels, r] = jnp.where(lane < DIL, a, source[0:channels, r])
            source[2 * channels : 3 * channels, r] = jnp.where(
                lane >= LANES - DIL, b, source[2 * channels : 3 * channels, r]
            )

    def transpose_in(src, src_row, dst, part, dst_row):
        v = jnp.transpose(src[:, src_row : src_row + DIL, :], (1, 0, 2))
        for h in range(DIL):
            dst[part : part + channels, lanes_of(dst_row + h)] = v[h]

    def transpose_out(value, dst, dst_row):
        v = jnp.stack([value[:, lanes_of(h)] for h in range(DIL)], axis=0)
        dst[:, dst_row : dst_row + DIL, :] = jnp.transpose(v, (1, 0, 2))

    center = slice(channels, 2 * channels)
    bias_sum = [jnp.zeros((channels, LANES), F32)]

    def forward_rows(r0, count):
        for r in range(r0, r0 + count, 8):
            z_val = offset
            for a in range(3):
                z_val = z_val + jnp.dot(
                    forward[a], stack[:, lanes_of(r + DIL * a, 8)], preferred_element_type=F32
                )
            value, slope = gelu_pair(z_val)
            act[:, lanes_of(r, 8)] = value.astype(BF16)
            g = (cot[:, lanes_of(r, 8)].astype(F32) * slope).astype(BF16)
            gstack[center, lanes_of(r + DIL, 8)] = g
            wide = g.astype(F32)
            part = bias_sum[0]
            for h in range(8):
                part = part + wide[:, lanes_of(h)]
            bias_sum[0] = part

    def weight_term(a, h0, count):
        return lax.dot_general(
            gstack[center, lanes_of(DIL + h0, count)],
            stack[:, lanes_of(h0 + DIL * a, count)],
            (((1,), (1,)), ((), ())),
            preferred_element_type=F32,
        )

    load_x.wait()
    for h in range(0, rows, DIL):
        transpose_in(xin, DIL + h, stack, channels, DIL + h)
    for g in range(groups):
        pack(stack, g)
    pl.semaphore_wait(barrier, len(greeted))

    xcopies = halo_copies(
        xin.at[:, DIL : 2 * DIL, :], xin.at[:, rows : rows + DIL, :],
        xin.at[:, 0:DIL, :], xin.at[:, rows + DIL : ext, :],
        xleft, xright, xsend, xrecv,
    )
    send(xcopies, ["u", "d", "l", "r", "ul", "ur", "dl", "dr"])
    for k in (3, -3):
        pl.semaphore_signal(chain_a, inc=1, device_id=deep(k), device_id_type=MESH)

    zero_edges(xleft, xright, xin.at[:, 0:DIL, :], xin.at[:, rows + DIL : ext, :])
    for h in range(rows):
        shift_row(stack, DIL + h)
    load_c.wait()
    for h in range(0, rows, DIL):
        transpose_in(cin, h, cot, 0, h)

    await_from(xcopies, ["l", "r"])
    for g in range(2, 2 + groups):
        merge_group(stack, xleft, xright, g)
    forward_rows(DIL, rows - 2 * DIL)
    inner = [weight_term(a, DIL, rows - 2 * DIL) for a in range(3)]
    for a in range(3):
        accs[a, :, 0 : 3 * channels] = inner[a]
    pl.semaphore_wait(chain_a, 2)
    for k in (2, -2):
        pl.semaphore_signal(chain_b, inc=1, device_id=deep(k), device_id_type=MESH)

    await_from(xcopies, ["u", "d", "ul", "ur", "dl", "dr"])
    for base, g0 in ((0, 0), (rows + DIL, 2 + groups)):
        transpose_in(xin, base, stack, channels, base)
        for h in range(DIL):
            shift_row(stack, base + h)
        for g in (g0, g0 + 1):
            merge_group(stack, xleft, xright, g)
    forward_rows(0, DIL)
    forward_rows(rows - DIL, DIL)
    await_sent(xcopies)
    for g in range(groups):
        pack(gstack, g)
    gcopies = halo_copies(
        gstack.at[center, lanes_of(DIL, DIL)], gstack.at[center, lanes_of(rows, DIL)],
        gstack.at[center, lanes_of(0, DIL)], gstack.at[center, lanes_of(rows + DIL, DIL)],
        gleft, gright, gsend, grecv,
    )
    send(gcopies, ["u", "d", "l", "r", "ul", "ur", "dl", "dr"])
    for a in range(3):
        accs[a, :, 0 : 3 * channels] += weight_term(a, 0, DIL) + weight_term(a, rows - DIL, DIL)
    accs[0, :, 3 * channels : 3 * channels + 1] = jnp.sum(bias_sum[0], axis=1, keepdims=True)
    for a in range(3):
        terms[:, 0, lanes_of(a)] = accs[a]

    def remote(src, dst, k, peer):
        pltpu.make_async_remote_copy(
            src, dst, rsend.at[k], rrecv.at[k], device_id=peer, device_id_type=MESH
        ).start()

    def drain(sem, buffer):
        pltpu.make_async_copy(buffer, buffer, sem).wait()

    for peer, index in plane:
        remote(terms.at[index], gathered.at[me], 0, peer)
    gathered[me] = terms[me]

    for h in range(0, rows, DIL):
        transpose_out(act[:, lanes_of(h, DIL)], act_c, h)
    store_a = pltpu.make_async_copy(act_c, act_out, local_sem.at[2])
    store_a.start()
    zero_edges(
        gleft, gright,
        gstack.at[center, lanes_of(0, DIL)], gstack.at[center, lanes_of(rows + DIL, DIL)],
    )
    for h in range(rows):
        shift_row(gstack, DIL + h)
    pl.semaphore_wait(chain_b, 2)

    drain(rrecv.at[0], gathered.at[pl.ds(0, PLANE - 1)])
    piece[0] = jnp.sum(gathered[...], axis=0)
    for k in ring_order(DEPTH):
        remote(piece.at[0], layers.at[z], 1, deep(k))
    layers[z] = piece[0]

    await_from(gcopies, names)
    for base in (0, rows + DIL):
        for h in range(DIL):
            shift_row(gstack, base + h)
    for g in range(4 + groups):
        merge_group(gstack, gleft, gright, g)
    for h in range(0, rows, DIL):
        tiles = []
        for r in (h, h + 8):
            out = None
            for a in range(3):
                d = jnp.dot(
                    backward[a], gstack[:, lanes_of(r + DIL * a, 8)], preferred_element_type=F32
                )
                out = d if out is None else out + d
            tiles.append(out.astype(BF16))
        transpose_out(jnp.concatenate(tiles, axis=1), grad_c, h)
    store_g = pltpu.make_async_copy(grad_c, grad_out, local_sem.at[3])
    store_g.start()

    drain(rrecv.at[1], layers.at[pl.ds(0, DEPTH - 1)])
    piece[1] = jnp.sum(layers[...], axis=0) * scale
    for peer, index in plane:
        remote(piece.at[1], total.at[me], 2, peer)
    total[me] = piece[1]
    await_sent(gcopies)
    store_a.wait()
    store_g.wait()
    drain(rsend.at[0], gathered.at[pl.ds(0, PLANE - 1)])
    drain(rsend.at[1], layers.at[pl.ds(0, DEPTH - 1)])
    drain(rrecv.at[2], total.at[pl.ds(0, PLANE - 1)])
    for a in range(3):
        tile = total[:, 0, lanes_of(a)]
        for e in range(3):
            gw_out[a, e] = tile[:, e * channels : (e + 1) * channels]
        if a == 0:
            column = tile[:, 3 * channels : 3 * channels + 1]
            gb_out[...] = jnp.sum(jnp.where(sub == lan, column, 0.0), axis=0, keepdims=True)
    drain(rsend.at[2], total.at[pl.ds(0, PLANE - 1)])


def shards(image, weight, bias, cotangent):
    channels, rows, columns = image.shape
    assert columns == LANES and rows % DIL == 0 and channels == PLANE
    count = rows * lax.axis_size("row") * columns * lax.axis_size("col")
    scale = 1.0 / math.sqrt(count)
    ext = rows + 2 * DIL
    groups = rows // 8
    vmem = pl.BlockSpec(memory_space=pltpu.VMEM)
    hbm = pl.BlockSpec(memory_space=pl.ANY)
    rim = pltpu.VMEM((groups + 4, channels, LANES), BF16)
    edge = pltpu.VMEM((groups, channels, LANES), BF16)
    tile = pltpu.VMEM((channels, rows, LANES), BF16)
    line = (1, 3 * LANES)

    def kernel(*refs):
        body(rows, scale, *refs)

    act, grad, gw, gb = pl.pallas_call(
        kernel,
        out_shape=(
            jax.ShapeDtypeStruct(image.shape, BF16),
            jax.ShapeDtypeStruct(image.shape, BF16),
            jax.ShapeDtypeStruct(weight.shape, F32),
            jax.ShapeDtypeStruct((1, channels), F32),
        ),
        in_specs=[hbm, vmem, vmem, hbm],
        out_specs=(hbm, hbm, vmem, vmem),
        scratch_shapes=[
            pltpu.VMEM((channels, ext, LANES), BF16),
            tile,
            pltpu.VMEM((channels, rows * LANES), BF16),
            pltpu.VMEM((3 * channels, ext * LANES), BF16),
            pltpu.VMEM((3 * channels, ext * LANES), BF16),
            rim, rim, rim, rim, edge, edge,
            pltpu.VMEM((channels, rows * LANES), BF16),
            tile, tile,
            pltpu.VMEM((3, channels, LANES), F32),
            pltpu.VMEM((PLANE,) + line, F32),
            pltpu.VMEM((PLANE,) + line, F32),
            pltpu.VMEM((DEPTH,) + line, F32),
            pltpu.VMEM((2,) + line, F32),
            pltpu.VMEM((PLANE,) + line, F32),
            pltpu.SemaphoreType.DMA((4,)),
            pltpu.SemaphoreType.DMA((8,)),
            pltpu.SemaphoreType.DMA((8,)),
            pltpu.SemaphoreType.DMA((8,)),
            pltpu.SemaphoreType.DMA((8,)),
            pltpu.SemaphoreType.DMA((3,)),
            pltpu.SemaphoreType.DMA((3,)),
            pltpu.SemaphoreType.REGULAR,
            pltpu.SemaphoreType.REGULAR,
        ],
        compiler_params=pltpu.CompilerParams(collective_id=0, has_side_effects=True),
    )(image, weight, bias.reshape(1, channels), cotangent)
    return act, grad, gw, gb.reshape(channels)


def solution(mesh):
    return jax.shard_map(
        shards,
        mesh=mesh,
        in_specs=(P(None, "row", "col"), P(), P(), P(None, "row", "col")),
        out_specs=(P(None, "row", "col"), P(None, "row", "col"), P(), P()),
        check_vma=False,
    )
```

time: 182 us -> 48.6 us (0.27)
  blocking collectives: 120 us -> 0 us
  Pallas kernels: 0 us -> 43.6 us
  starting transfers between devices: 26.7 us -> 0 us
  local copies, waits for them, and re-layouts: 18.2 us -> 4.14 us
  waiting for transfers between devices: 6.11 us -> 0 us
  matrix products: 5.82 us -> 0 us
  other arithmetic: 3.41 us -> 0 us
    psum x1 -> x0, blocking collectives: 120 us -> none  [shards(): lax.psum((local_weight, local_bias), ('row', 'col'))]
    pallas_call x0 -> x1, Pallas kernels: none -> 43.6 us  [shards(): pl.pallas_call(kernel, out_shape=(jax.ShapeDtypeStruct(image.shape, BF16)...]
    ppermute x8 -> x0, starting transfers between devices: 26.7 us -> none  [from_behind(): lax.ppermute(value, axis, [(source, source + steps) for source in range(i...]
    ppermute x8 -> x0, waiting for transfers between devices: 6.11 us -> none  [from_behind(): lax.ppermute(value, axis, [(source, source + steps) for source in range(i...]
    slice x10 -> x0, local copies, waits for them, and re-layouts: 6.06 us -> none  [the longest x3 1.95 us: extended(): tall_block[:, :, column_count - DILATION_PIXELS:]]
    dot_general x9 -> x0, matrix products: 5.82 us -> none  [the longest x3 2.79 us: shards(): jnp.einsum('ok,krq->orq', weight_row, stacked, preferred_element_type=jnp...]
    ppermute x4 -> x0, local copies, waits for them, and re-layouts: 4.41 us -> none  [from_behind(): lax.ppermute(value, axis, [(source, source + steps) for source in range(i...]
    concatenate x4 -> x0, other arithmetic: 3.35 us -> none  [the longest x2 2.62 us: extended(): return jnp.concatenate([left_margin, tall_block, right_margin], axis=2)]
  transfers between devices with their start and end apart: 8 -> 0, of which waited for: 4 -> 0; matrix products, arithmetic and copies ran while one was open for 4% -> 0% of each run, Pallas kernels for 0% -> 0%
where the time goes in v2:
time: 48.6 us; the launch traced here: 48.4 us
  Pallas kernels  43.6 us (90%)
  local copies, waits for them, and re-layouts  4.14 us (9%)
  between operations  0.65 us (1%)
    pallas_call x1, Pallas kernels, shards(): pl.pallas_call(kernel, out_shape=(jax.ShapeDtypeStruct(image.shape, BF16)...  43.6 us
    unnamed x10, local copies, waits for them, and re-layouts  4.14 us

profile of v2, /device:TPU:1, one launch (start us, length us, event | category | flops | bytes accessed | tf_op | source)
XLA Modules:
  0.0 48.4 jit_solution(11885120355068048869)
XLA Ops:
  0.6 43.6 %shard_map.75 = (bf16[32,64,128]{2,1,0:T(8,128)(2,1)}, bf16[32,64,128]{2,1,0:T(8,128)(2,1)}, f32[3,3,32,32]{3,2,1,0:T(8,128)}, f32[1,32]{1,0:T(1,128)}) custom-call(bf16[32,64,128]{2,1,0:T(8,128)(2,1)} %refs_0_.1, bf16[3,3,32,32]{3,2,1,0:T(8,128)(2,1)} %refs_1_.1, f32[1,32]{1,0:T(1,128)} %bitcast.2, bf16[32,64,128]{2,1,0:T(8,128)(2,1)} %refs_3_.1), custom_call_target="tpu_custom_call" | custom-call | tf_op jit(solution)/shard_map/pallas_call | solution.py:370
  44.3 0.0 copy-start
  44.3 1.9 %copy.12 = bf16[32,64,128]{2,1,0:T(8,128)(2,1)} copy(bf16[32,64,128]{2,1,0:T(8,128)(2,1)} %get-tuple-element.16) | data formatting | bytes 1048576
  46.2 0.0 copy-done
  46.2 0.0 copy-start.1
  46.2 0.8 %copy.13 = bf16[32,64,128]{2,1,0:T(8,128)(2,1)} copy(bf16[32,64,128]{2,1,0:T(8,128)(2,1)S(1)} %copy-done) | data formatting | bytes 1048576
  47.0 0.2 copy-done.1
  47.2 0.0 copy-start.2
  47.2 0.7 %copy.14 = f32[3,3,32,32]{3,2,1,0:T(8,128)} copy(f32[3,3,32,32]{3,2,1,0:T(8,128)S(1)} %copy-done.1) | data formatting | bytes 73728
  47.9 0.0 copy-done.2
  47.9 0.5 %copy.15 = f32[32]{0:T(128)} copy(f32[32]{0:T(128)S(1)} %bitcast.3) | data formatting | bytes 256
Async XLA Ops:
  44.3 1.9 %copy-start = (bf16[32,64,128]{2,1,0:T(8,128)(2,1)S(1)}, bf16[32,64,128]{2,1,0:T(8,128)(2,1)}, u32[]{:S(2)}) copy-start(bf16[32,64,128]{2,1,0:T(8,128)(2,1)} %get-tuple-element.17) | copy-start | bytes 1572868
  46.2 1.0 %copy-start.1 = (f32[3,3,32,32]{3,2,1,0:T(8,128)S(1)}, f32[3,3,32,32]{3,2,1,0:T(8,128)}, u32[]{:S(2)}) copy-start(f32[3,3,32,32]{3,2,1,0:T(8,128)} %get-tuple-element.18) | copy-start | bytes 110596
  47.2 0.7 %copy-start.2 = (f32[1,32]{1,0:T(1,128)S(1)}, f32[1,32]{1,0:T(1,128)}, u32[]{:S(2)}) copy-start(f32[1,32]{1,0:T(1,128)} %get-tuple-element.11) | copy-start | bytes 388

commit v3 on v2

--- a/solution.py
+++ b/solution.py
@@ -36,11 +36,11 @@
 
 def body(
     rows, scale,
-    image, weight, bias, cotangent,
-    act_out, grad_out, gw_out, gb_out,
-    xin, cin, cot, stack, gstack, xleft, xright, gleft, gright,
-    pack_l, pack_r, act, act_c, grad_c, accs,
-    terms, gathered, layers, piece, total,
+    image, weight_in, bias_in, cotangent,
+    act_c, grad_c, total,
+    weight, bias, xin, cin, cot, stack, gstack, xleft, xright, gleft, gright,
+    pack_l, pack_r, act, accs,
+    terms, gathered, layers, piece,
     local_sem, xsend, xrecv, gsend, grecv, rsend, rrecv, chain_a, chain_b,
 ):
     channels = image.shape[0]
@@ -71,30 +71,21 @@
         plane.append(({"row": (py % 2) * DEPTH + z, "col": pcol}, (py % 2) * 16 + pcol))
 
     barrier = pltpu.get_barrier_semaphore()
-    near = [at(-1, 0), at(1, 0), at(-1, -1), at(-1, 1), at(1, -1), at(1, 1)]
-    near += [deep(k) for k in (3, -3, 2, -2, 1, -1)]
-    greeted = near + [peer for peer, _ in plane]
+    greeted = [at(-1, 0), at(1, 0), at(0, -1), at(0, 1), at(-1, -1), at(-1, 1), at(1, -1), at(1, 1)]
+    greeted += [deep(k) for k in (2, -2, 1, -1)]
+    greeted += [peer for (peer, _), o in zip(plane, offsets) if hops(o[0]) + hops(o[1]) <= 2]
     for peer in greeted:
         pl.semaphore_signal(barrier, inc=1, device_id=peer, device_id_type=MESH)
 
     load_x = pltpu.make_async_copy(image, xin.at[:, DIL : DIL + rows, :], local_sem.at[0])
     load_c = pltpu.make_async_copy(cotangent, cin, local_sem.at[1])
-    load_x.start()
-    load_c.start()
+    load_w = pltpu.make_async_copy(weight_in, weight, local_sem.at[2])
+    load_b = pltpu.make_async_copy(bias_in, bias, local_sem.at[3])
+    for load in (load_x, load_w, load_b, load_c):
+        load.start()
 
     lane = lax.broadcasted_iota(jnp.int32, (channels, LANES), 1)
     slot = lane // DIL
-    forward = [
-        jnp.concatenate([weight[a, e] for e in range(3)], axis=1) for a in range(3)
-    ]
-    backward = [
-        jnp.concatenate([weight[2 - a, 2 - e].T for e in range(3)], axis=1) for a in range(3)
-    ]
-    sub = lax.broadcasted_iota(jnp.int32, (channels, channels), 0)
-    lan = lax.broadcasted_iota(jnp.int32, (channels, channels), 1)
-    offset = jnp.sum(jnp.where(sub == lan, bias[...], 0.0), axis=1, keepdims=True)
-    accs[...] = jnp.zeros_like(accs)
-
     top, bottom = row == 0, row == nrow - 1
     first, last = col == 0, col == ncol - 1
     has = {
@@ -103,16 +94,25 @@
         "dl": (row < nrow - 1) & (col > 0), "dr": (row < nrow - 1) & (col < ncol - 1),
     }
     step = {
-        "u": (-1, 0), "d": (1, 0), "l": (0, -1), "r": (0, 1),
+        "u0": (-1, 0), "d0": (1, 0), "u1": (-1, 0), "d1": (1, 0), "l": (0, -1), "r": (0, 1),
         "ul": (-1, -1), "ur": (-1, 1), "dl": (1, -1), "dr": (1, 1),
     }
-    mirror = {"u": "d", "d": "u", "l": "r", "r": "l", "ul": "dr", "dr": "ul", "ur": "dl", "dl": "ur"}
+    mirror = {
+        "u0": "d0", "d0": "u0", "u1": "d1", "d1": "u1", "l": "r", "r": "l",
+        "ul": "dr", "dr": "ul", "ur": "dl", "dl": "ur",
+    }
+    for n in ("u0", "u1", "d0", "d1"):
+        has[n] = has[n[0]]
     names = list(step)
+    vertical = ["d0", "u0", "d1", "u1"]
+    sideways = ["l", "r", "ul", "ur", "dl", "dr"]
 
     def halo_copies(top_src, bottom_src, top_dst, bottom_dst, left, right, send, recv):
         src_dst = {
-            "u": (top_src, bottom_dst),
-            "d": (bottom_src, top_dst),
+            "u0": (top_src(0), bottom_dst(0)),
+            "u1": (top_src(1), bottom_dst(1)),
+            "d0": (bottom_src(0), top_dst(0)),
+            "d1": (bottom_src(1), top_dst(1)),
             "l": (pack_l, right.at[2 : 2 + groups]),
             "r": (pack_r, left.at[2 : 2 + groups]),
             "ul": (pack_l.at[0:2], right.at[2 + groups : 4 + groups]),
@@ -184,9 +184,9 @@
                 lane >= LANES - DIL, b, source[2 * channels : 3 * channels, r]
             )
 
-    def transpose_in(src, src_row, dst, part, dst_row):
-        v = jnp.transpose(src[:, src_row : src_row + DIL, :], (1, 0, 2))
-        for h in range(DIL):
+    def transpose_in(src, src_row, dst, part, dst_row, count=DIL):
+        v = jnp.transpose(src[:, src_row : src_row + count, :], (1, 0, 2))
+        for h in range(count):
             dst[part : part + channels, lanes_of(dst_row + h)] = v[h]
 
     def transpose_out(value, dst, dst_row):
@@ -221,21 +221,29 @@
             preferred_element_type=F32,
         )
 
+    def rows_of(ref, r0):
+        return lambda k: ref.at[:, r0 + 8 * k : r0 + 8 * k + 8, :]
+
+    def lines_of(r0):
+        return lambda k: gstack.at[center, lanes_of(r0 + 8 * k, 8)]
+
+    pl.semaphore_wait(barrier, len(greeted))
+    xcopies = halo_copies(
+        rows_of(image, 0), rows_of(image, rows - DIL), rows_of(xin, 0), rows_of(xin, rows + DIL),
+        xleft, xright, xsend, xrecv,
+    )
+    send(xcopies, vertical)
+
     load_x.wait()
     for h in range(0, rows, DIL):
         transpose_in(xin, DIL + h, stack, channels, DIL + h)
     for g in range(groups):
         pack(stack, g)
-    pl.semaphore_wait(barrier, len(greeted))
-
-    xcopies = halo_copies(
-        xin.at[:, DIL : 2 * DIL, :], xin.at[:, rows : rows + DIL, :],
-        xin.at[:, 0:DIL, :], xin.at[:, rows + DIL : ext, :],
-        xleft, xright, xsend, xrecv,
-    )
-    send(xcopies, ["u", "d", "l", "r", "ul", "ur", "dl", "dr"])
-    for k in (3, -3):
-        pl.semaphore_signal(chain_a, inc=1, device_id=deep(k), device_id_type=MESH)
+    send(xcopies, sideways)
+    chain = [peer for (peer, _), o in zip(plane, offsets) if o[0] % 2 and o[1] % 2 and o[2] == 0]
+    chain += [deep(2), deep(-2)]
+    for peer in chain:
+        pl.semaphore_signal(chain_a, inc=1, device_id=peer, device_id_type=MESH)
 
     zero_edges(xleft, xright, xin.at[:, 0:DIL, :], xin.at[:, rows + DIL : ext, :])
     for h in range(rows):
@@ -243,41 +251,45 @@
     load_c.wait()
     for h in range(0, rows, DIL):
         transpose_in(cin, h, cot, 0, h)
+    load_w.wait()
+    load_b.wait()
+    forward = [
+        jnp.concatenate([weight[a, e] for e in range(3)], axis=1) for a in range(3)
+    ]
+    backward = [
+        jnp.concatenate([weight[2 - a, 2 - e].T for e in range(3)], axis=1) for a in range(3)
+    ]
+    sub = lax.broadcasted_iota(jnp.int32, (channels, channels), 0)
+    lan = lax.broadcasted_iota(jnp.int32, (channels, channels), 1)
+    offset = jnp.sum(jnp.where(sub == lan, bias[...], 0.0), axis=1, keepdims=True)
+    accs[...] = jnp.zeros_like(accs)
+
 
     await_from(xcopies, ["l", "r"])
     for g in range(2, 2 + groups):
         merge_group(stack, xleft, xright, g)
     forward_rows(DIL, rows - 2 * DIL)
     inner = [weight_term(a, DIL, rows - 2 * DIL) for a in range(3)]
+
+    for k in range(2):
+        await_from(xcopies, [f"u{k}", f"d{k}"] + (["ul", "ur", "dl", "dr"] if k == 0 else []))
+        for base, g in ((8 * k, k), (rows + DIL + 8 * k, 2 + groups + k)):
+            transpose_in(xin, base, stack, channels, base, 8)
+            for h in range(8):
+                shift_row(stack, base + h)
+            merge_group(stack, xleft, xright, g)
+        for r in (8 * k, rows - DIL + 8 * k):
+            forward_rows(r, 8)
+            for a in range(3):
+                inner[a] = inner[a] + weight_term(a, r, 8)
     for a in range(3):
         accs[a, :, 0 : 3 * channels] = inner[a]
-    pl.semaphore_wait(chain_a, 2)
-    for k in (2, -2):
-        pl.semaphore_signal(chain_b, inc=1, device_id=deep(k), device_id_type=MESH)
-
-    await_from(xcopies, ["u", "d", "ul", "ur", "dl", "dr"])
-    for base, g0 in ((0, 0), (rows + DIL, 2 + groups)):
-        transpose_in(xin, base, stack, channels, base)
-        for h in range(DIL):
-            shift_row(stack, base + h)
-        for g in (g0, g0 + 1):
-            merge_group(stack, xleft, xright, g)
-    forward_rows(0, DIL)
-    forward_rows(rows - DIL, DIL)
-    await_sent(xcopies)
-    for g in range(groups):
-        pack(gstack, g)
-    gcopies = halo_copies(
-        gstack.at[center, lanes_of(DIL, DIL)], gstack.at[center, lanes_of(rows, DIL)],
-        gstack.at[center, lanes_of(0, DIL)], gstack.at[center, lanes_of(rows + DIL, DIL)],
-        gleft, gright, gsend, grecv,
-    )
-    send(gcopies, ["u", "d", "l", "r", "ul", "ur", "dl", "dr"])
-    for a in range(3):
-        accs[a, :, 0 : 3 * channels] += weight_term(a, 0, DIL) + weight_term(a, rows - DIL, DIL)
     accs[0, :, 3 * channels : 3 * channels + 1] = jnp.sum(bias_sum[0], axis=1, keepdims=True)
     for a in range(3):
         terms[:, 0, lanes_of(a)] = accs[a]
+    pl.semaphore_wait(chain_a, len(chain))
+    for k in (4, -4):
+        pl.semaphore_signal(chain_b, inc=1, device_id=deep(k), device_id_type=MESH)
 
     def remote(src, dst, k, peer):
         pltpu.make_async_remote_copy(
@@ -291,14 +303,20 @@
         remote(terms.at[index], gathered.at[me], 0, peer)
     gathered[me] = terms[me]
 
-    for h in range(0, rows, DIL):
-        transpose_out(act[:, lanes_of(h, DIL)], act_c, h)
-    store_a = pltpu.make_async_copy(act_c, act_out, local_sem.at[2])
-    store_a.start()
+    await_sent(xcopies)
+    gcopies = halo_copies(
+        lines_of(DIL), lines_of(rows), lines_of(0), lines_of(rows + DIL), gleft, gright, gsend, grecv,
+    )
+    send(gcopies, vertical)
+    for g in range(groups):
+        pack(gstack, g)
+    send(gcopies, sideways)
     zero_edges(
         gleft, gright,
         gstack.at[center, lanes_of(0, DIL)], gstack.at[center, lanes_of(rows + DIL, DIL)],
     )
+    for h in range(0, rows, DIL):
+        transpose_out(act[:, lanes_of(h, DIL)], act_c, h)
     for h in range(rows):
         shift_row(gstack, DIL + h)
     pl.semaphore_wait(chain_b, 2)
@@ -326,8 +344,6 @@
                 out = d if out is None else out + d
             tiles.append(out.astype(BF16))
         transpose_out(jnp.concatenate(tiles, axis=1), grad_c, h)
-    store_g = pltpu.make_async_copy(grad_c, grad_out, local_sem.at[3])
-    store_g.start()
 
     drain(rrecv.at[1], layers.at[pl.ds(0, DEPTH - 1)])
     piece[1] = jnp.sum(layers[...], axis=0) * scale
@@ -335,11 +351,22 @@
         remote(piece.at[1], total.at[me], 2, peer)
     total[me] = piece[1]
     await_sent(gcopies)
-    store_a.wait()
-    store_g.wait()
     drain(rsend.at[0], gathered.at[pl.ds(0, PLANE - 1)])
     drain(rsend.at[1], layers.at[pl.ds(0, DEPTH - 1)])
     drain(rrecv.at[2], total.at[pl.ds(0, PLANE - 1)])
+    drain(rsend.at[2], total.at[pl.ds(0, PLANE - 1)])
+
+
+def write_out(act_c, grad_c, total, act_out, grad_out, gw_out, gb_out, sem):
+    channels = act_c.shape[0]
+    copies = [
+        pltpu.make_async_copy(act_c, act_out, sem.at[0]),
+        pltpu.make_async_copy(grad_c, grad_out, sem.at[1]),
+    ]
+    for copy in copies:
+        copy.start()
+    sub = lax.broadcasted_iota(jnp.int32, (channels, channels), 0)
+    lan = lax.broadcasted_iota(jnp.int32, (channels, channels), 1)
     for a in range(3):
         tile = total[:, 0, lanes_of(a)]
         for e in range(3):
@@ -347,7 +374,8 @@
         if a == 0:
             column = tile[:, 3 * channels : 3 * channels + 1]
             gb_out[...] = jnp.sum(jnp.where(sub == lan, column, 0.0), axis=0, keepdims=True)
-    drain(rsend.at[2], total.at[pl.ds(0, PLANE - 1)])
+    for copy in copies:
+        copy.wait()
 
 
 def shards(image, weight, bias, cotangent):
@@ -358,7 +386,7 @@
     ext = rows + 2 * DIL
     groups = rows // 8
     vmem = pl.BlockSpec(memory_space=pltpu.VMEM)
-    hbm = pl.BlockSpec(memory_space=pl.ANY)
+    hbm = pl.BlockSpec(memory_space=pltpu.HBM)
     rim = pltpu.VMEM((groups + 4, channels, LANES), BF16)
     edge = pltpu.VMEM((groups, channels, LANES), BF16)
     tile = pltpu.VMEM((channels, rows, LANES), BF16)
@@ -367,17 +395,18 @@
     def kernel(*refs):
         body(rows, scale, *refs)
 
-    act, grad, gw, gb = pl.pallas_call(
+    act_c, grad_c, total = pl.pallas_call(
         kernel,
         out_shape=(
             jax.ShapeDtypeStruct(image.shape, BF16),
             jax.ShapeDtypeStruct(image.shape, BF16),
-            jax.ShapeDtypeStruct(weight.shape, F32),
-            jax.ShapeDtypeStruct((1, channels), F32),
+            jax.ShapeDtypeStruct((PLANE,) + line, F32),
         ),
-        in_specs=[hbm, vmem, vmem, hbm],
-        out_specs=(hbm, hbm, vmem, vmem),
+        in_specs=[hbm] * 4,
+        out_specs=(vmem, vmem, vmem),
         scratch_shapes=[
+            pltpu.VMEM(weight.shape, BF16),
+            pltpu.VMEM((1, channels), F32),
             pltpu.VMEM((channels, ext, LANES), BF16),
             tile,
             pltpu.VMEM((channels, rows * LANES), BF16),
@@ -385,25 +414,38 @@
             pltpu.VMEM((3 * channels, ext * LANES), BF16),
             rim, rim, rim, rim, edge, edge,
             pltpu.VMEM((channels, rows * LANES), BF16),
-            tile, tile,
             pltpu.VMEM((3, channels, LANES), F32),
             pltpu.VMEM((PLANE,) + line, F32),
             pltpu.VMEM((PLANE,) + line, F32),
             pltpu.VMEM((DEPTH,) + line, F32),
             pltpu.VMEM((2,) + line, F32),
-            pltpu.VMEM((PLANE,) + line, F32),
             pltpu.SemaphoreType.DMA((4,)),
-            pltpu.SemaphoreType.DMA((8,)),
-            pltpu.SemaphoreType.DMA((8,)),
-            pltpu.SemaphoreType.DMA((8,)),
-            pltpu.SemaphoreType.DMA((8,)),
+            pltpu.SemaphoreType.DMA((10,)),
+            pltpu.SemaphoreType.DMA((10,)),
+            pltpu.SemaphoreType.DMA((10,)),
+            pltpu.SemaphoreType.DMA((10,)),
             pltpu.SemaphoreType.DMA((3,)),
             pltpu.SemaphoreType.DMA((3,)),
             pltpu.SemaphoreType.REGULAR,
             pltpu.SemaphoreType.REGULAR,
         ],
-        compiler_params=pltpu.CompilerParams(collective_id=0, has_side_effects=True),
-    )(image, weight, bias.reshape(1, channels), cotangent)
+        compiler_params=pltpu.CompilerParams(
+            collective_id=0, has_side_effects=True, vmem_limit_bytes=20 * 2**20
+        ),
+    )(*(pltpu.with_memory_space_constraint(v, pltpu.HBM) for v in (image, weight, bias.reshape(1, channels), cotangent)))
+    act, grad, gw, gb = pl.pallas_call(
+        write_out,
+        out_shape=(
+            jax.ShapeDtypeStruct(image.shape, BF16),
+            jax.ShapeDtypeStruct(image.shape, BF16),
+            jax.ShapeDtypeStruct(weight.shape, F32),
+            jax.ShapeDtypeStruct((1, channels), F32),
+        ),
+        in_specs=[vmem] * 3,
+        out_specs=(hbm, hbm, vmem, vmem),
+        scratch_shapes=[pltpu.SemaphoreType.DMA((2,))],
+        compiler_params=pltpu.CompilerParams(vmem_limit_bytes=8 * 2**20),
+    )(act_c, grad_c, total)
     return act, grad, gw, gb.reshape(channels)
 
 

time: 48.6 us -> 45.1 us (0.928)
  local copies, waits for them, and re-layouts: 4.14 us -> 0 us
  Pallas kernels: 43.6 us -> 44.3 us
    unnamed x10 -> x0, local copies, waits for them, and re-layouts: 4.14 us -> none
    pallas_call x0 -> x1, Pallas kernels: none -> 1.67 us  [shards(): pl.pallas_call(write_out, out_shape=(jax.ShapeDtypeStruct(image.shape, BF...]
    pallas_call x1, Pallas kernels: 43.6 us -> 42.7 us  [shards(): pl.pallas_call(kernel, out_shape=(jax.ShapeDtypeStruct(image.shape, BF16)...]
where the time goes in v3:
time: 45.1 us; the launch traced here: 45 us
  Pallas kernels  44.3 us (98%)
  between operations  0.64 us (1%)
    pallas_call x1, Pallas kernels, shards(): pl.pallas_call(kernel, out_shape=(jax.ShapeDtypeStruct(image.shape, BF16)...  42.7 us
    pallas_call x1, Pallas kernels, shards(): pl.pallas_call(write_out, out_shape=(jax.ShapeDtypeStruct(image.shape, BF...  1.67 us

profile of v3, /device:TPU:1, one launch (start us, length us, event | category | flops | bytes accessed | tf_op | source)
XLA Modules:
  0.0 45.0 jit_solution(16531223722373604588)
XLA Ops:
  0.6 42.7 %shard_map.75 = (bf16[32,64,128]{2,1,0:T(8,128)(2,1)S(1)}, bf16[32,64,128]{2,1,0:T(8,128)(2,1)S(1)}, f32[32,1,384]{2,1,0:T(1,128)S(1)}) custom-call(bf16[32,64,128]{2,1,0:T(8,128)(2,1)} %refs_0_.1, bf16[3,3,32,32]{3,2,1,0:T(8,128)(2,1)} %refs_1_.1, f32[1,32]{1,0:T(1,128)} %bitcast.2, bf16[32,64,128]{2,1,0:T(8,128)(2,1)} %refs_3_.1), custom_call_target="tpu_custom_call" | custom-call | tf_op jit(solution)/shard_map/pallas_call | solution.py:398
  43.3 1.7 %shard_map.76 = (bf16[32,64,128]{2,1,0:T(8,128)(2,1)}, bf16[32,64,128]{2,1,0:T(8,128)(2,1)}, f32[3,3,32,32]{3,2,1,0:T(8,128)}, f32[1,32]{1,0:T(1,128)}) custom-call(bf16[32,64,128]{2,1,0:T(8,128)(2,1)S(1)} %get-tuple-element.11.act_c, bf16[32,64,128]{2,1,0:T(8,128)(2,1)S(1)} %get-tuple-element.12.grad_c, f32[32,1,384]{2,1,0:T(1,128)S(1)} %get-tuple-element.13.total), custom_call_target="tpu_custom_call" | custom-call | tf_op jit(solution)/shard_map/pallas_call | solution.py:436

commit v4 on v3

--- a/solution.py
+++ b/solution.py
@@ -39,7 +39,7 @@
     image, weight_in, bias_in, cotangent,
     act_c, grad_c, total,
     weight, bias, xin, cin, cot, stack, gstack, xleft, xright, gleft, gright,
-    pack_l, pack_r, act, accs,
+    cot_l, cot_r, act_l, act_r, grad_l, grad_r, act, accs,
     terms, gathered, layers, piece,
     local_sem, xsend, xrecv, gsend, grecv, rsend, rrecv, chain_a, chain_b,
 ):
@@ -71,7 +71,7 @@
         plane.append(({"row": (py % 2) * DEPTH + z, "col": pcol}, (py % 2) * 16 + pcol))
 
     barrier = pltpu.get_barrier_semaphore()
-    greeted = [at(-1, 0), at(1, 0), at(0, -1), at(0, 1), at(-1, -1), at(-1, 1), at(1, -1), at(1, 1)]
+    greeted = [at(0, -1), at(0, 1), at(-1, 0), at(1, 0), at(-1, -1), at(-1, 1), at(1, -1), at(1, 1)]
     greeted += [deep(k) for k in (2, -2, 1, -1)]
     greeted += [peer for (peer, _), o in zip(plane, offsets) if hops(o[0]) + hops(o[1]) <= 2]
     for peer in greeted:
@@ -107,18 +107,22 @@
     vertical = ["d0", "u0", "d1", "u1"]
     sideways = ["l", "r", "ul", "ur", "dl", "dr"]
 
-    def halo_copies(top_src, bottom_src, top_dst, bottom_dst, left, right, send, recv):
+    low, center, high = (slice(k * channels, (k + 1) * channels) for k in range(3))
+    above, below = lanes_of(0, 2), lanes_of(2 + groups, 2)
+    level = lanes_of(2, groups)
+
+    def halo_copies(top_src, bottom_src, top_dst, bottom_dst, own_l, own_r, left, right, send, recv):
         src_dst = {
             "u0": (top_src(0), bottom_dst(0)),
             "u1": (top_src(1), bottom_dst(1)),
             "d0": (bottom_src(0), top_dst(0)),
             "d1": (bottom_src(1), top_dst(1)),
-            "l": (pack_l, right.at[2 : 2 + groups]),
-            "r": (pack_r, left.at[2 : 2 + groups]),
-            "ul": (pack_l.at[0:2], right.at[2 + groups : 4 + groups]),
-            "ur": (pack_r.at[0:2], left.at[2 + groups : 4 + groups]),
-            "dl": (pack_l.at[groups - 2 : groups], right.at[0:2]),
-            "dr": (pack_r.at[groups - 2 : groups], left.at[0:2]),
+            "l": (own_l(0, groups), right.at[:, level]),
+            "r": (own_r(0, groups), left.at[:, level]),
+            "ul": (own_l(0, 2), right.at[:, below]),
+            "ur": (own_r(0, 2), left.at[:, below]),
+            "dl": (own_l(groups - 2, 2), right.at[:, above]),
+            "dr": (own_r(groups - 2, 2), left.at[:, above]),
         }
         return {
             n: pltpu.make_async_remote_copy(
@@ -141,116 +145,153 @@
     def await_sent(copies):
         when_each(names, lambda n: has[n], lambda n: copies[n].wait_send())
 
+    def clear(ref):
+        ref[...] = jnp.zeros(ref.shape, ref.dtype)
+
     def zero_edges(left, right, top_dst, bottom_dst):
-        pl.when(first)(lambda: left.__setitem__(Ellipsis, jnp.zeros_like(left)))
-        pl.when(last)(lambda: right.__setitem__(Ellipsis, jnp.zeros_like(right)))
+        pl.when(first)(lambda: clear(left))
+        pl.when(last)(lambda: clear(right))
 
         @pl.when(top)
         def _():
-            top_dst[...] = jnp.zeros(top_dst.shape, BF16)
-            left[0:2] = jnp.zeros((2,) + left.shape[1:], BF16)
-            right[0:2] = jnp.zeros((2,) + left.shape[1:], BF16)
+            clear(top_dst)
+            clear(left.at[:, above])
+            clear(right.at[:, above])
 
         @pl.when(bottom)
         def _():
-            bottom_dst[...] = jnp.zeros(bottom_dst.shape, BF16)
-            left[2 + groups : 4 + groups] = jnp.zeros((2,) + left.shape[1:], BF16)
-            right[2 + groups : 4 + groups] = jnp.zeros((2,) + left.shape[1:], BF16)
-
-    def pack(source, g):
-        lefts, rights = None, None
+            clear(bottom_dst)
+            clear(left.at[:, below])
+            clear(right.at[:, below])
+
+    def pack(source, part, r, column, target, to, g):
+        merged = None
         for k in range(8):
-            v = source[channels : 2 * channels, lanes_of(DIL + 8 * g + k)]
-            a = v if k == 0 else pltpu.roll(v, DIL * k, 1)
-            b = v if k == 7 else pltpu.roll(v, DIL * k + DIL, 1)
-            lefts = a if k == 0 else jnp.where(slot == k, a, lefts)
-            rights = b if k == 0 else jnp.where(slot == k, b, rights)
-        pack_l[g] = lefts
-        pack_r[g] = rights
+            v = source[part, lanes_of(r + k)]
+            turn = (DIL * k - column) % LANES
+            v = pltpu.roll(v, turn, 1) if turn else v
+            merged = v if merged is None else jnp.where(slot == k, v, merged)
+        target[to, lanes_of(g)] = merged
+
+    def unpack(target, part, r, left, right, g, k):
+        a, b = left[:, lanes_of(g)], right[:, lanes_of(g)]
+        a = pltpu.roll(a, LANES - DIL * k, 1) if k else a
+        b = pltpu.roll(b, LANES - DIL - DIL * k, 1) if k < 7 else b
+        v = target[part, lanes_of(r)]
+        target[part, lanes_of(r)] = jnp.where(lane < DIL, a, jnp.where(lane >= LANES - DIL, b, v))
 
     def shift_row(source, r):
-        v = source[channels : 2 * channels, lanes_of(r)]
-        source[0:channels, lanes_of(r)] = pltpu.roll(v, DIL, 1)
-        source[2 * channels : 3 * channels, lanes_of(r)] = pltpu.roll(v, LANES - DIL, 1)
+        v = source[center, lanes_of(r)]
+        source[low, lanes_of(r)] = pltpu.roll(v, DIL, 1)
+        source[high, lanes_of(r)] = pltpu.roll(v, LANES - DIL, 1)
 
     def merge_group(source, left, right, g):
-        lv, rv = left[g], right[g]
+        lv, rv = left[:, lanes_of(g)], right[:, lanes_of(g)]
         for k in range(8):
             r = lanes_of(8 * g + k)
             a = lv if k == 0 else pltpu.roll(lv, LANES - DIL * k, 1)
             b = rv if k == 7 else pltpu.roll(rv, LANES - DIL - DIL * k, 1)
-            source[0:channels, r] = jnp.where(lane < DIL, a, source[0:channels, r])
-            source[2 * channels : 3 * channels, r] = jnp.where(
-                lane >= LANES - DIL, b, source[2 * channels : 3 * channels, r]
-            )
+            source[low, r] = jnp.where(lane < DIL, a, source[low, r])
+            source[high, r] = jnp.where(lane >= LANES - DIL, b, source[high, r])
 
     def transpose_in(src, src_row, dst, part, dst_row, count=DIL):
         v = jnp.transpose(src[:, src_row : src_row + count, :], (1, 0, 2))
         for h in range(count):
-            dst[part : part + channels, lanes_of(dst_row + h)] = v[h]
+            dst[part, lanes_of(dst_row + h)] = v[h]
 
     def transpose_out(value, dst, dst_row):
         v = jnp.stack([value[:, lanes_of(h)] for h in range(DIL)], axis=0)
         dst[:, dst_row : dst_row + DIL, :] = jnp.transpose(v, (1, 0, 2))
 
-    center = slice(channels, 2 * channels)
     bias_sum = [jnp.zeros((channels, LANES), F32)]
 
+    def pixels(source, offsets, count, factor):
+        z_val = offset
+        for a in range(3):
+            z_val = z_val + jnp.dot(
+                forward[a], source[:, lanes_of(offsets[a], count)], preferred_element_type=F32
+            )
+        value, slope = gelu_pair(z_val)
+        g = (factor.astype(F32) * slope).astype(BF16)
+        wide = g.astype(F32)
+        part = bias_sum[0]
+        for h in range(count):
+            part = part + wide[:, lanes_of(h)]
+        bias_sum[0] = part
+        return value.astype(BF16), g
+
     def forward_rows(r0, count):
-        for r in range(r0, r0 + count, 8):
-            z_val = offset
+        for r in range(r0, r0 + count, 4):
+            value, g = pixels(stack, [r + DIL * a for a in range(3)], 4, cot[:, lanes_of(r, 4)])
+            act[:, lanes_of(r, 4)] = value
+            gstack[center, lanes_of(r + DIL, 4)] = g
+
+    sides = ((xleft, cot_l, act_l, grad_l), (xright, cot_r, act_r, grad_r))
+
+    def forward_edges(g0, count):
+        for source, factor, value_to, grad_to in sides:
+            for g in range(g0, g0 + count, 2):
+                value, grad = pixels(source, [g + 2 * a for a in range(3)], 2, factor[:, lanes_of(g, 2)])
+                value_to[:, lanes_of(g, 2)] = value
+                grad_to[:, lanes_of(g, 2)] = grad
+
+    def pixel_sum(left, right):
+        return lax.dot_general(left, right, (((1,), (1,)), ((), ())), preferred_element_type=F32)
+
+    def weight_rows(h0, count):
+        for a in range(3):
+            inner[a] = inner[a] + pixel_sum(
+                gstack[center, lanes_of(DIL + h0, count)], stack[:, lanes_of(h0 + DIL * a, count)]
+            )
+
+    def weight_edges(g0, count):
+        for source, _, _, grad in sides:
             for a in range(3):
-                z_val = z_val + jnp.dot(
-                    forward[a], stack[:, lanes_of(r + DIL * a, 8)], preferred_element_type=F32
+                inner[a] = inner[a] + pixel_sum(
+                    grad[:, lanes_of(g0, count)], source[:, lanes_of(g0 + 2 * a, count)]
                 )
-            value, slope = gelu_pair(z_val)
-            act[:, lanes_of(r, 8)] = value.astype(BF16)
-            g = (cot[:, lanes_of(r, 8)].astype(F32) * slope).astype(BF16)
-            gstack[center, lanes_of(r + DIL, 8)] = g
-            wide = g.astype(F32)
-            part = bias_sum[0]
-            for h in range(8):
-                part = part + wide[:, lanes_of(h)]
-            bias_sum[0] = part
-
-    def weight_term(a, h0, count):
-        return lax.dot_general(
-            gstack[center, lanes_of(DIL + h0, count)],
-            stack[:, lanes_of(h0 + DIL * a, count)],
-            (((1,), (1,)), ((), ())),
-            preferred_element_type=F32,
-        )
 
     def rows_of(ref, r0):
         return lambda k: ref.at[:, r0 + 8 * k : r0 + 8 * k + 8, :]
 
     def lines_of(r0):
         return lambda k: gstack.at[center, lanes_of(r0 + 8 * k, 8)]
+
+    load_x.wait()
+    for h in range(0, rows, DIL):
+        transpose_in(xin, DIL + h, stack, center, DIL + h)
+    for g in range(groups):
+        pack(stack, center, DIL + 8 * g, 0, xleft, center, 2 + g)
+        pack(stack, center, DIL + 8 * g, LANES - DIL, xright, center, 2 + g)
 
     pl.semaphore_wait(barrier, len(greeted))
     xcopies = halo_copies(
         rows_of(image, 0), rows_of(image, rows - DIL), rows_of(xin, 0), rows_of(xin, rows + DIL),
-        xleft, xright, xsend, xrecv,
+        lambda g, n: xleft.at[center, lanes_of(2 + g, n)],
+        lambda g, n: xright.at[center, lanes_of(2 + g, n)],
+        xleft.at[low], xright.at[high], xsend, xrecv,
     )
-    send(xcopies, vertical)
-
-    load_x.wait()
-    for h in range(0, rows, DIL):
-        transpose_in(xin, DIL + h, stack, channels, DIL + h)
-    for g in range(groups):
-        pack(stack, g)
-    send(xcopies, sideways)
+    send(xcopies, sideways[:2] + vertical + sideways[2:])
     chain = [peer for (peer, _), o in zip(plane, offsets) if o[0] % 2 and o[1] % 2 and o[2] == 0]
     chain += [deep(2), deep(-2)]
     for peer in chain:
         pl.semaphore_signal(chain_a, inc=1, device_id=peer, device_id_type=MESH)
 
-    zero_edges(xleft, xright, xin.at[:, 0:DIL, :], xin.at[:, rows + DIL : ext, :])
+    zero_edges(
+        xleft.at[low], xright.at[high], xin.at[:, 0:DIL, :], xin.at[:, rows + DIL : ext, :]
+    )
     for h in range(rows):
         shift_row(stack, DIL + h)
     load_c.wait()
     for h in range(0, rows, DIL):
-        transpose_in(cin, h, cot, 0, h)
+        transpose_in(cin, h, cot, slice(0, channels), h)
+    for g in range(groups):
+        pack(cot, slice(0, channels), 8 * g, 0, cot_l, slice(0, channels), g)
+        pack(cot, slice(0, channels), 8 * g, LANES - DIL, cot_r, slice(0, channels), g)
+    inside = (lane >= DIL) & (lane < LANES - DIL)
+    for h in range(rows):
+        v = cot[:, lanes_of(h)]
+        cot[:, lanes_of(h)] = jnp.where(inside, v, jnp.zeros_like(v))
     load_w.wait()
     load_b.wait()
     forward = [
@@ -265,23 +306,49 @@
     accs[...] = jnp.zeros_like(accs)
 
 
-    await_from(xcopies, ["l", "r"])
-    for g in range(2, 2 + groups):
-        merge_group(stack, xleft, xright, g)
     forward_rows(DIL, rows - 2 * DIL)
-    inner = [weight_term(a, DIL, rows - 2 * DIL) for a in range(3)]
-
-    for k in range(2):
-        await_from(xcopies, [f"u{k}", f"d{k}"] + (["ul", "ur", "dl", "dr"] if k == 0 else []))
+    blocks = [gstack[center, lanes_of(DIL + h, DIL)] for h in range(DIL, rows - DIL, DIL)]
+    none = jnp.zeros_like(blocks[0])
+    stacked = None
+    for k in range(len(blocks) + 2):
+        lines = [blocks[k - a] if 0 <= k - a < len(blocks) else none for a in range(3)]
+        d = lax.dot_general(
+            jnp.concatenate(lines, axis=0),
+            stack[:, lanes_of((k + 1) * DIL, DIL)],
+            (((1,), (1,)), ((), ())),
+            preferred_element_type=F32,
+        )
+        stacked = d if stacked is None else stacked + d
+    inner = [stacked[a * channels : (a + 1) * channels] for a in range(3)]
+
+    for g in range(groups):
+        pack(stack, center, DIL + 8 * g, DIL, xleft, high, 2 + g)
+        pack(stack, center, DIL + 8 * g, LANES - 2 * DIL, xright, low, 2 + g)
+
+    def rim(k):
+        await_from(xcopies, [f"u{k}", f"d{k}"])
         for base, g in ((8 * k, k), (rows + DIL + 8 * k, 2 + groups + k)):
-            transpose_in(xin, base, stack, channels, base, 8)
+            transpose_in(xin, base, stack, center, base, 8)
             for h in range(8):
                 shift_row(stack, base + h)
-            merge_group(stack, xleft, xright, g)
         for r in (8 * k, rows - DIL + 8 * k):
             forward_rows(r, 8)
-            for a in range(3):
-                inner[a] = inner[a] + weight_term(a, r, 8)
+            weight_rows(r, 8)
+        for base, g in ((8 * k, k), (rows + DIL + 8 * k, 2 + groups + k)):
+            pack(stack, center, base, 0, xleft, center, g)
+            pack(stack, center, base, DIL, xleft, high, g)
+            pack(stack, center, base, LANES - 2 * DIL, xright, low, g)
+            pack(stack, center, base, LANES - DIL, xright, center, g)
+
+    rim(0)
+    await_from(xcopies, ["l", "r"])
+    forward_edges(2, groups - 4)
+    weight_edges(2, groups - 4)
+    rim(1)
+    await_from(xcopies, ["ul", "ur", "dl", "dr"])
+    for g in (0, groups - 2):
+        forward_edges(g, 2)
+        weight_edges(g, 2)
     for a in range(3):
         accs[a, :, 0 : 3 * channels] = inner[a]
     accs[0, :, 3 * channels : 3 * channels + 1] = jnp.sum(bias_sum[0], axis=1, keepdims=True)
@@ -303,14 +370,21 @@
         remote(terms.at[index], gathered.at[me], 0, peer)
     gathered[me] = terms[me]
 
-    await_sent(xcopies)
     gcopies = halo_copies(
-        lines_of(DIL), lines_of(rows), lines_of(0), lines_of(rows + DIL), gleft, gright, gsend, grecv,
+        lines_of(DIL), lines_of(rows), lines_of(0), lines_of(rows + DIL),
+        lambda g, n: grad_l.at[:, lanes_of(g, n)],
+        lambda g, n: grad_r.at[:, lanes_of(g, n)],
+        gleft, gright, gsend, grecv,
     )
-    send(gcopies, vertical)
-    for g in range(groups):
-        pack(gstack, g)
     send(gcopies, sideways)
+    rim_first = [r for r in range(rows) if r < DIL or r >= rows - DIL]
+    rim_first += [r for r in range(DIL, rows - DIL)]
+    for n, r in enumerate(rim_first):
+        unpack(gstack, center, DIL + r, grad_l, grad_r, r // 8, r % 8)
+        if n == 2 * DIL - 1:
+            send(gcopies, vertical)
+    for r in range(rows):
+        unpack(act, slice(0, channels), r, act_l, act_r, r // 8, r % 8)
     zero_edges(
         gleft, gright,
         gstack.at[center, lanes_of(0, DIL)], gstack.at[center, lanes_of(rows + DIL, DIL)],
@@ -350,6 +424,7 @@
     for peer, index in plane:
         remote(piece.at[1], total.at[me], 2, peer)
     total[me] = piece[1]
+    await_sent(xcopies)
     await_sent(gcopies)
     drain(rsend.at[0], gathered.at[pl.ds(0, PLANE - 1)])
     drain(rsend.at[1], layers.at[pl.ds(0, DEPTH - 1)])
@@ -357,23 +432,27 @@
     drain(rsend.at[2], total.at[pl.ds(0, PLANE - 1)])
 
 
-def write_out(act_c, grad_c, total, act_out, grad_out, gw_out, gb_out, sem):
+def write_out(act_c, grad_c, total, act_out, grad_out, gw_out, gb_out, gw, gb, sem):
     channels = act_c.shape[0]
     copies = [
         pltpu.make_async_copy(act_c, act_out, sem.at[0]),
         pltpu.make_async_copy(grad_c, grad_out, sem.at[1]),
+        pltpu.make_async_copy(gw, gw_out, sem.at[2]),
+        pltpu.make_async_copy(gb, gb_out, sem.at[3]),
     ]
-    for copy in copies:
-        copy.start()
+    copies[0].start()
+    copies[1].start()
     sub = lax.broadcasted_iota(jnp.int32, (channels, channels), 0)
     lan = lax.broadcasted_iota(jnp.int32, (channels, channels), 1)
     for a in range(3):
         tile = total[:, 0, lanes_of(a)]
         for e in range(3):
-            gw_out[a, e] = tile[:, e * channels : (e + 1) * channels]
+            gw[a, e] = tile[:, e * channels : (e + 1) * channels]
         if a == 0:
             column = tile[:, 3 * channels : 3 * channels + 1]
-            gb_out[...] = jnp.sum(jnp.where(sub == lan, column, 0.0), axis=0, keepdims=True)
+            gb[...] = jnp.sum(jnp.where(sub == lan, column, 0.0), axis=0, keepdims=True)
+    copies[2].start()
+    copies[3].start()
     for copy in copies:
         copy.wait()
 
@@ -387,8 +466,9 @@
     groups = rows // 8
     vmem = pl.BlockSpec(memory_space=pltpu.VMEM)
     hbm = pl.BlockSpec(memory_space=pltpu.HBM)
-    rim = pltpu.VMEM((groups + 4, channels, LANES), BF16)
-    edge = pltpu.VMEM((groups, channels, LANES), BF16)
+    taps = pltpu.VMEM((3 * channels, (groups + 4) * LANES), BF16)
+    rim = pltpu.VMEM((channels, (groups + 4) * LANES), BF16)
+    edge = pltpu.VMEM((channels, groups * LANES), BF16)
     tile = pltpu.VMEM((channels, rows, LANES), BF16)
     line = (1, 3 * LANES)
 
@@ -412,7 +492,7 @@
             pltpu.VMEM((channels, rows * LANES), BF16),
             pltpu.VMEM((3 * channels, ext * LANES), BF16),
             pltpu.VMEM((3 * channels, ext * LANES), BF16),
-            rim, rim, rim, rim, edge, edge,
+            taps, taps, rim, rim, edge, edge, edge, edge, edge, edge,
             pltpu.VMEM((channels, rows * LANES), BF16),
             pltpu.VMEM((3, channels, LANES), F32),
             pltpu.VMEM((PLANE,) + line, F32),
@@ -442,8 +522,12 @@
             jax.ShapeDtypeStruct((1, channels), F32),
         ),
         in_specs=[vmem] * 3,
-        out_specs=(hbm, hbm, vmem, vmem),
-        scratch_shapes=[pltpu.SemaphoreType.DMA((2,))],
+        out_specs=(hbm, hbm, hbm, hbm),
+        scratch_shapes=[
+            pltpu.VMEM(weight.shape, F32),
+            pltpu.VMEM((1, channels), F32),
+            pltpu.SemaphoreType.DMA((4,)),
+        ],
         compiler_params=pltpu.CompilerParams(vmem_limit_bytes=8 * 2**20),
     )(act_c, grad_c, total)
     return act, grad, gw, gb.reshape(channels)

time: 45.1 us -> 42.2 us (0.936)
  Pallas kernels: 44.3 us -> 41.5 us
    pallas_call x1, Pallas kernels: 42.7 us -> 40.4 us  [shards(): pl.pallas_call(kernel, out_shape=(jax.ShapeDtypeStruct(image.shape, BF16)...]
    pallas_call x1, Pallas kernels: 1.67 us -> 1.05 us  [shards(): pl.pallas_call(write_out, out_shape=(jax.ShapeDtypeStruct(image.shape, BF...]
where the time goes in v4:
time: 42.2 us; the launch traced here: 42.1 us
  Pallas kernels  41.5 us (98%)
  between operations  0.64 us (2%)
    pallas_call x1, Pallas kernels, shards(): pl.pallas_call(kernel, out_shape=(jax.ShapeDtypeStruct(image.shape, BF16)...  40.4 us
    pallas_call x1, Pallas kernels, shards(): pl.pallas_call(write_out, out_shape=(jax.ShapeDtypeStruct(image.shape, BF...  1.05 us

profile of v4, /device:TPU:1, one launch (start us, length us, event | category | flops | bytes accessed | tf_op | source)
XLA Modules:
  0.0 42.1 jit_solution(17083202402942157072)
XLA Ops:
  0.6 40.4 %shard_map.75 = (bf16[32,64,128]{2,1,0:T(8,128)(2,1)S(1)}, bf16[32,64,128]{2,1,0:T(8,128)(2,1)S(1)}, f32[32,1,384]{2,1,0:T(1,128)S(1)}) custom-call(bf16[32,64,128]{2,1,0:T(8,128)(2,1)} %refs_0_.1, bf16[3,3,32,32]{3,2,1,0:T(8,128)(2,1)} %refs_1_.1, f32[1,32]{1,0:T(1,128)} %bitcast.2, bf16[32,64,128]{2,1,0:T(8,128)(2,1)} %refs_3_.1), custom_call_target="tpu_custom_call" | custom-call | tf_op jit(solution)/shard_map/pallas_call | solution.py:478
  41.0 1.1 %shard_map.76 = (bf16[32,64,128]{2,1,0:T(8,128)(2,1)}, bf16[32,64,128]{2,1,0:T(8,128)(2,1)}, f32[3,3,32,32]{3,2,1,0:T(8,128)}, f32[1,32]{1,0:T(1,128)}) custom-call(bf16[32,64,128]{2,1,0:T(8,128)(2,1)S(1)} %get-tuple-element.11.act_c, bf16[32,64,128]{2,1,0:T(8,128)(2,1)S(1)} %get-tuple-element.12.grad_c, f32[32,1,384]{2,1,0:T(1,128)S(1)} %get-tuple-element.13.total), custom_call_target="tpu_custom_call" | custom-call | tf_op jit(solution)/shard_map/pallas_call | solution.py:516

commit v5 on v4

--- a/solution.py
+++ b/solution.py
@@ -38,11 +38,15 @@
     rows, scale,
     image, weight_in, bias_in, cotangent,
     act_c, grad_c, total,
-    weight, bias, xin, cin, cot, stack, gstack, xleft, xright, gleft, gright,
-    cot_l, cot_r, act_l, act_r, grad_l, grad_r, act, accs,
+    weight, bias, xin, cin, cot, stack, gstack, xside, gleft, gright,
+    cot_s, act_s, grad_s, act, accs,
     terms, gathered, layers, piece,
-    local_sem, xsend, xrecv, gsend, grecv, rsend, rrecv, chain_a, chain_b,
+    local_sem, xsend, xrecv, gsend, grecv, rsend, rrecv, chain_a, chain_b, chain_c,
 ):
+    xleft, xright = xside.at[0], xside.at[1]
+    cot_l, cot_r = cot_s.at[0], cot_s.at[1]
+    act_l, act_r = act_s.at[0], act_s.at[1]
+    grad_l, grad_r = grad_s.at[0], grad_s.at[1]
     channels = image.shape[0]
     ext = rows + 2 * DIL
     groups = rows // 8
@@ -71,7 +75,8 @@
         plane.append(({"row": (py % 2) * DEPTH + z, "col": pcol}, (py % 2) * 16 + pcol))
 
     barrier = pltpu.get_barrier_semaphore()
-    greeted = [at(0, -1), at(0, 1), at(-1, 0), at(1, 0), at(-1, -1), at(-1, 1), at(1, -1), at(1, 1)]
+    beside = [at(-1, 0), at(1, 0)]
+    greeted = [at(0, -1), at(0, 1)] + beside
     greeted += [deep(k) for k in (2, -2, 1, -1)]
     greeted += [peer for (peer, _), o in zip(plane, offsets) if hops(o[0]) + hops(o[1]) <= 2]
     for peer in greeted:
@@ -226,14 +231,14 @@
             act[:, lanes_of(r, 4)] = value
             gstack[center, lanes_of(r + DIL, 4)] = g
 
-    sides = ((xleft, cot_l, act_l, grad_l), (xright, cot_r, act_r, grad_r))
-
-    def forward_edges(g0, count):
-        for source, factor, value_to, grad_to in sides:
-            for g in range(g0, g0 + count, 2):
-                value, grad = pixels(source, [g + 2 * a for a in range(3)], 2, factor[:, lanes_of(g, 2)])
-                value_to[:, lanes_of(g, 2)] = value
-                grad_to[:, lanes_of(g, 2)] = grad
+    early, late = 1 - core, core
+
+    def forward_edges(side, g0, count):
+        source, factor = xside.at[side], cot_s.at[side]
+        for g in range(g0, g0 + count, 2):
+            value, grad = pixels(source, [g + 2 * a for a in range(3)], 2, factor[:, lanes_of(g, 2)])
+            act_s[side, :, lanes_of(g, 2)] = value
+            grad_s[side, :, lanes_of(g, 2)] = grad
 
     def pixel_sum(left, right):
         return lax.dot_general(left, right, (((1,), (1,)), ((), ())), preferred_element_type=F32)
@@ -244,12 +249,11 @@
                 gstack[center, lanes_of(DIL + h0, count)], stack[:, lanes_of(h0 + DIL * a, count)]
             )
 
-    def weight_edges(g0, count):
-        for source, _, _, grad in sides:
-            for a in range(3):
-                inner[a] = inner[a] + pixel_sum(
-                    grad[:, lanes_of(g0, count)], source[:, lanes_of(g0 + 2 * a, count)]
-                )
+    def weight_edges(side, g0, count):
+        for a in range(3):
+            inner[a] = inner[a] + pixel_sum(
+                grad_s[side, :, lanes_of(g0, count)], xside[side, :, lanes_of(g0 + 2 * a, count)]
+            )
 
     def rows_of(ref, r0):
         return lambda k: ref.at[:, r0 + 8 * k : r0 + 8 * k + 8, :]
@@ -271,7 +275,9 @@
         lambda g, n: xright.at[center, lanes_of(2 + g, n)],
         xleft.at[low], xright.at[high], xsend, xrecv,
     )
-    send(xcopies, sideways[:2] + vertical + sideways[2:])
+    for peer in beside:
+        pl.semaphore_signal(chain_c, inc=1, device_id=peer, device_id_type=MESH)
+    send(xcopies, sideways[:2] + vertical)
     chain = [peer for (peer, _), o in zip(plane, offsets) if o[0] % 2 and o[1] % 2 and o[2] == 0]
     chain += [deep(2), deep(-2)]
     for peer in chain:
@@ -282,6 +288,8 @@
     )
     for h in range(rows):
         shift_row(stack, DIL + h)
+    pl.semaphore_wait(chain_c, len(beside))
+    send(xcopies, sideways[2:])
     load_c.wait()
     for h in range(0, rows, DIL):
         transpose_in(cin, h, cot, slice(0, channels), h)
@@ -340,15 +348,23 @@
             pack(stack, center, base, LANES - 2 * DIL, xright, low, g)
             pack(stack, center, base, LANES - DIL, xright, center, g)
 
+    def await_side(right):
+        pl.when(right & has["r"])(lambda: xcopies[mirror["r"]].wait_recv())
+        pl.when(jnp.logical_not(right) & has["l"])(lambda: xcopies[mirror["l"]].wait_recv())
+
     rim(0)
-    await_from(xcopies, ["l", "r"])
-    forward_edges(2, groups - 4)
-    weight_edges(2, groups - 4)
+    await_side(early == 1)
+    forward_edges(early, 2, groups - 4)
+    weight_edges(early, 2, groups - 4)
     rim(1)
+    await_side(late == 1)
+    forward_edges(late, 2, groups - 4)
+    weight_edges(late, 2, groups - 4)
     await_from(xcopies, ["ul", "ur", "dl", "dr"])
-    for g in (0, groups - 2):
-        forward_edges(g, 2)
-        weight_edges(g, 2)
+    for side in (0, 1):
+        for g in (0, groups - 2):
+            forward_edges(side, g, 2)
+            weight_edges(side, g, 2)
     for a in range(3):
         accs[a, :, 0 : 3 * channels] = inner[a]
     accs[0, :, 3 * channels : 3 * channels + 1] = jnp.sum(bias_sum[0], axis=1, keepdims=True)
@@ -466,9 +482,9 @@
     groups = rows // 8
     vmem = pl.BlockSpec(memory_space=pltpu.VMEM)
     hbm = pl.BlockSpec(memory_space=pltpu.HBM)
-    taps = pltpu.VMEM((3 * channels, (groups + 4) * LANES), BF16)
+    taps = pltpu.VMEM((2, 3 * channels, (groups + 4) * LANES), BF16)
     rim = pltpu.VMEM((channels, (groups + 4) * LANES), BF16)
-    edge = pltpu.VMEM((channels, groups * LANES), BF16)
+    edge = pltpu.VMEM((2, channels, groups * LANES), BF16)
     tile = pltpu.VMEM((channels, rows, LANES), BF16)
     line = (1, 3 * LANES)
 
@@ -492,7 +508,7 @@
             pltpu.VMEM((channels, rows * LANES), BF16),
             pltpu.VMEM((3 * channels, ext * LANES), BF16),
             pltpu.VMEM((3 * channels, ext * LANES), BF16),
-            taps, taps, rim, rim, edge, edge, edge, edge, edge, edge,
+            taps, rim, rim, edge, edge, edge,
             pltpu.VMEM((channels, rows * LANES), BF16),
             pltpu.VMEM((3, channels, LANES), F32),
             pltpu.VMEM((PLANE,) + line, F32),
@@ -506,6 +522,7 @@
             pltpu.SemaphoreType.DMA((10,)),
             pltpu.SemaphoreType.DMA((3,)),
             pltpu.SemaphoreType.DMA((3,)),
+            pltpu.SemaphoreType.REGULAR,
             pltpu.SemaphoreType.REGULAR,
             pltpu.SemaphoreType.REGULAR,
         ],

time: 42.2 us -> 41.3 us (0.979)
  Pallas kernels: 41.5 us -> 40.6 us
    pallas_call x1, Pallas kernels: 40.4 us -> 39.5 us  [shards(): pl.pallas_call(kernel, out_shape=(jax.ShapeDtypeStruct(image.shape, BF16)...]
where the time goes in v5:
time: 41.3 us; the launch traced here: 41.2 us
  Pallas kernels  40.6 us (98%)
  between operations  0.64 us (2%)
    pallas_call x1, Pallas kernels, shards(): pl.pallas_call(kernel, out_shape=(jax.ShapeDtypeStruct(image.shape, BF16)...  39.5 us
    pallas_call x1, Pallas kernels, shards(): pl.pallas_call(write_out, out_shape=(jax.ShapeDtypeStruct(image.shape, BF...  1.05 us

profile of v5, /device:TPU:1, one launch (start us, length us, event | category | flops | bytes accessed | tf_op | source)
XLA Modules:
  0.0 41.2 jit_solution(2318222328348212043)
XLA Ops:
  0.6 39.5 %shard_map.75 = (bf16[32,64,128]{2,1,0:T(8,128)(2,1)S(1)}, bf16[32,64,128]{2,1,0:T(8,128)(2,1)S(1)}, f32[32,1,384]{2,1,0:T(1,128)S(1)}) custom-call(bf16[32,64,128]{2,1,0:T(8,128)(2,1)} %refs_0_.1, bf16[3,3,32,32]{3,2,1,0:T(8,128)(2,1)} %refs_1_.1, f32[1,32]{1,0:T(1,128)} %bitcast.2, bf16[32,64,128]{2,1,0:T(8,128)(2,1)} %refs_3_.1), custom_call_target="tpu_custom_call" | custom-call | tf_op jit(solution)/shard_map/pallas_call | solution.py:494
  40.1 1.1 %shard_map.76 = (bf16[32,64,128]{2,1,0:T(8,128)(2,1)}, bf16[32,64,128]{2,1,0:T(8,128)(2,1)}, f32[3,3,32,32]{3,2,1,0:T(8,128)}, f32[1,32]{1,0:T(1,128)}) custom-call(bf16[32,64,128]{2,1,0:T(8,128)(2,1)S(1)} %get-tuple-element.11.act_c, bf16[32,64,128]{2,1,0:T(8,128)(2,1)S(1)} %get-tuple-element.12.grad_c, f32[32,1,384]{2,1,0:T(1,128)S(1)} %get-tuple-element.13.total), custom_call_target="tpu_custom_call" | custom-call | tf_op jit(solution)/shard_map/pallas_call | solution.py:533

commit v6 on v5

--- a/solution.py
+++ b/solution.py
@@ -41,7 +41,7 @@
     weight, bias, xin, cin, cot, stack, gstack, xside, gleft, gright,
     cot_s, act_s, grad_s, act, accs,
     terms, gathered, layers, piece,
-    local_sem, xsend, xrecv, gsend, grecv, rsend, rrecv, chain_a, chain_b, chain_c,
+    local_sem, xsend, xrecv, gsend, grecv, rsend, rrecv, chain_a, chain_b, chain_c, chain_d,
 ):
     xleft, xright = xside.at[0], xside.at[1]
     cot_l, cot_r = cot_s.at[0], cot_s.at[1]
@@ -77,8 +77,8 @@
     barrier = pltpu.get_barrier_semaphore()
     beside = [at(-1, 0), at(1, 0)]
     greeted = [at(0, -1), at(0, 1)] + beside
-    greeted += [deep(k) for k in (2, -2, 1, -1)]
-    greeted += [peer for (peer, _), o in zip(plane, offsets) if hops(o[0]) + hops(o[1]) <= 2]
+    greeted += [deep(k) for k in (1, -1)]
+    greeted += [peer for (peer, _), o in zip(plane, offsets) if hops(o[0]) + hops(o[1]) <= 1]
     for peer in greeted:
         pl.semaphore_signal(barrier, inc=1, device_id=peer, device_id_type=MESH)
 
@@ -275,20 +275,24 @@
         lambda g, n: xright.at[center, lanes_of(2 + g, n)],
         xleft.at[low], xright.at[high], xsend, xrecv,
     )
+    adjacent = [peer for (peer, _), o in zip(plane, offsets) if hops(o[0]) + hops(o[1]) == 1 and o[2] == 0]
+    adjacent += [deep(1), deep(-1)]
+    for peer in adjacent:
+        pl.semaphore_signal(chain_d, inc=1, device_id=peer, device_id_type=MESH)
     for peer in beside:
         pl.semaphore_signal(chain_c, inc=1, device_id=peer, device_id_type=MESH)
     send(xcopies, sideways[:2] + vertical)
-    chain = [peer for (peer, _), o in zip(plane, offsets) if o[0] % 2 and o[1] % 2 and o[2] == 0]
-    chain += [deep(2), deep(-2)]
-    for peer in chain:
-        pl.semaphore_signal(chain_a, inc=1, device_id=peer, device_id_type=MESH)
-
     zero_edges(
         xleft.at[low], xright.at[high], xin.at[:, 0:DIL, :], xin.at[:, rows + DIL : ext, :]
     )
     for h in range(rows):
         shift_row(stack, DIL + h)
     pl.semaphore_wait(chain_c, len(beside))
+    pl.semaphore_wait(chain_d, len(adjacent))
+    chain = [peer for (peer, _), o in zip(plane, offsets) if o[0] % 2 and o[1] % 2 and o[2] == 0]
+    chain += [deep(2), deep(-2)]
+    for peer in chain:
+        pl.semaphore_signal(chain_a, inc=1, device_id=peer, device_id_type=MESH)
     send(xcopies, sideways[2:])
     load_c.wait()
     for h in range(0, rows, DIL):
@@ -525,6 +529,7 @@
             pltpu.SemaphoreType.REGULAR,
             pltpu.SemaphoreType.REGULAR,
             pltpu.SemaphoreType.REGULAR,
+            pltpu.SemaphoreType.REGULAR,
         ],
         compiler_params=pltpu.CompilerParams(
             collective_id=0, has_side_effects=True, vmem_limit_bytes=20 * 2**20

time: 41.3 us -> 41.1 us (level)
  no operation moved by 1% of the time
where the time goes in v6:
time: 41.1 us; the launch traced here: 41 us
  Pallas kernels  40.3 us (98%)
  between operations  0.64 us (2%)
    pallas_call x1, Pallas kernels, shards(): pl.pallas_call(kernel, out_shape=(jax.ShapeDtypeStruct(image.shape, BF16)...  39.3 us
    pallas_call x1, Pallas kernels, shards(): pl.pallas_call(write_out, out_shape=(jax.ShapeDtypeStruct(image.shape, BF...  1.05 us

profile of v6, /device:TPU:1, one launch (start us, length us, event | category | flops | bytes accessed | tf_op | source)
XLA Modules:
  0.0 41.0 jit_solution(14799603865121548390)
XLA Ops:
  0.6 39.3 %shard_map.75 = (bf16[32,64,128]{2,1,0:T(8,128)(2,1)S(1)}, bf16[32,64,128]{2,1,0:T(8,128)(2,1)S(1)}, f32[32,1,384]{2,1,0:T(1,128)S(1)}) custom-call(bf16[32,64,128]{2,1,0:T(8,128)(2,1)} %refs_0_.1, bf16[3,3,32,32]{3,2,1,0:T(8,128)(2,1)} %refs_1_.1, f32[1,32]{1,0:T(1,128)} %bitcast.2, bf16[32,64,128]{2,1,0:T(8,128)(2,1)} %refs_3_.1), custom_call_target="tpu_custom_call" | custom-call | tf_op jit(solution)/shard_map/pallas_call | solution.py:498
  39.9 1.1 %shard_map.76 = (bf16[32,64,128]{2,1,0:T(8,128)(2,1)}, bf16[32,64,128]{2,1,0:T(8,128)(2,1)}, f32[3,3,32,32]{3,2,1,0:T(8,128)}, f32[1,32]{1,0:T(1,128)}) custom-call(bf16[32,64,128]{2,1,0:T(8,128)(2,1)S(1)} %get-tuple-element.11.act_c, bf16[32,64,128]{2,1,0:T(8,128)(2,1)S(1)} %get-tuple-element.12.grad_c, f32[32,1,384]{2,1,0:T(1,128)S(1)} %get-tuple-element.13.total), custom_call_target="tpu_custom_call" | custom-call | tf_op jit(solution)/shard_map/pallas_call | solution.py:538
